TPU v7x, 128 devices: a whole 4x4x4 slice. The times are simulated.
128 devices in a mesh: rows: 16 (over x, y), cols: 8 (over z, core).
Axes of the slice: x: 4, y: 4, z: 4, core: 2. Of those that a mesh axis runs over, the one named last changes fastest.
Arguments:
- trace: float32 [32, 8388608], P(None, ('rows', 'cols')), may hold values from -4 to 4
- selectors: int32 [33, 8388608], P(None, ('rows', 'cols')), may hold values 0 or 1
- mds: float32 [32, 32], replicated, may hold values from -1 to 1
- quad: float32 [32], replicated, may hold values from -0.5 to 0.5
- alpha: float32 [33], replicated, may hold values from -1 to 1
- challenges: float32 [2], replicated, may hold values from 0.3 to 0.6
- divisor_inv: float32 [8388608], P(('rows', 'cols')), may hold values from 0.5 to 2
- hash_mds: float32 [12, 12], replicated, may hold values from -6 to 6
- hash_rc: float32 [2, 12], replicated, may hold values from -1 to 1
Outputs:
- digests: float32 [4, 16, 524288], P(None, None, ('rows', 'cols'))
All inputs are finite; a program needn't handle non-finite values. No bound on the sum of `selectors` on one device may be relied on, other than what follows from the above.
Results may differ from a plain program's by a relative error of at most 0.00035.
Values sent between devices are 32-bit elements; how exact they have to be, the bound alone decides.
A program may use at most 192 MiB of HBM per device.

v0:
```python
import math

import jax
import jax.numpy as jnp
from jax import lax
from jax.sharding import PartitionSpec as P

BLOWUP = 8
SEGMENTS = 8
DIGEST = 4
ROUNDS = 2


highest = lax.Precision.HIGHEST


def from_behind(array, axis, by):
    count = lax.axis_size(axis)
    return lax.ppermute(array, axis, [(i, (i + by) % count) for i in range(count)])


def entering(value, axis, join, neutral):
    count, mine = (lax.axis_size(axis), lax.axis_index(axis))
    pieces = lax.all_gather(value, axis)
    subtotal = jnp.full_like(value, 0) + jnp.asarray(neutral, value.dtype)

    def turn(position, subtotal):
        longer = join(subtotal, pieces[position])
        return jnp.where(position < mine, longer, subtotal)

    return lax.fori_loop(0, count - 1, turn, subtotal)


def squash(value):
    return value * lax.rsqrt(1.0 + value * value)


def permute(state, hash_mds, hash_rc):
    for step in range(ROUNDS):
        state = (
            jnp.dot(hash_mds, squash(state), precision=highest, preferred_element_type=jnp.float32)
            + hash_rc[step][:, None]
        )
    return state


def turns(product, modulus, sign):
    angle = sign * 2.0 * math.pi / modulus * (product % modulus).astype(jnp.float32)
    return (jnp.cos(angle), jnp.sin(angle))


def complex_mul(left_re, left_im, right_re, right_im):
    return (left_re * right_re - left_im * right_im, left_re * right_im + left_im * right_re)


def local_dft(values_re, values_im, sign):
    length = values_re.shape[-1]
    first = 128
    second = length // first
    leading = values_re.shape[:-1]
    block_re = values_re.reshape(leading + (first, second))
    block_im = values_im.reshape(leading + (first, second))
    index_one = jnp.arange(first, dtype=jnp.int32)
    index_two = jnp.arange(second, dtype=jnp.int32)
    cos_one, sin_one = turns(index_one[:, None] * index_one[None, :], first, sign)
    section_re = jnp.einsum("kn,...nm->...km", cos_one, block_re, precision=highest) - jnp.einsum(
        "kn,...nm->...km", sin_one, block_im, precision=highest
    )
    section_im = jnp.einsum("kn,...nm->...km", cos_one, block_im, precision=highest) + jnp.einsum(
        "kn,...nm->...km", sin_one, block_re, precision=highest
    )
    twist_cos, twist_sin = turns(index_one[:, None] * index_two[None, :], length, sign)
    section_re, section_im = complex_mul(section_re, section_im, twist_cos, twist_sin)
    cos_two, sin_two = turns(index_two[:, None] * index_two[None, :], second, sign)
    final_re = jnp.einsum("...kn,jn->...kj", section_re, cos_two, precision=highest) - jnp.einsum(
        "...kn,jn->...kj", section_im, sin_two, precision=highest
    )
    final_im = jnp.einsum("...kn,jn->...kj", section_re, sin_two, precision=highest) + jnp.einsum(
        "...kn,jn->...kj", section_im, cos_two, precision=highest
    )
    final_re = jnp.swapaxes(final_re, -1, -2).reshape(leading + (length,))
    final_im = jnp.swapaxes(final_im, -1, -2).reshape(leading + (length,))
    return (final_re, final_im)


def regroup(values):
    return lax.all_to_all(values, ("rows", "cols"), split_axis=1, concat_axis=1, tiled=True)


def column_relay(values):
    return lax.all_to_all(values, "cols", split_axis=1, concat_axis=1, tiled=True)


def add_terms(earlier, later):
    return earlier + later


def on_device(trace, selectors, mds, quad, alpha, challenges, divisor_inv, hash_mds, hash_rc):
    width = trace.shape[0]
    rows_dev = trace.shape[1]
    n_rows = lax.axis_size("rows")
    n_cols = lax.axis_size("cols")
    devices = n_rows * n_cols
    total_rows = rows_dev * devices
    flat_index = lax.axis_index(("rows", "cols"))
    row_index = lax.axis_index("rows")
    rim = from_behind(trace[:, :BLOWUP], ("rows", "cols"), -1)
    extended = jnp.concatenate([trace, rim], axis=1)
    following = extended[:, BLOWUP:]
    linear = jnp.dot(mds, trace, precision=highest, preferred_element_type=jnp.float32)
    cons = following - linear - quad[:, None] * trace * trace
    step_size = challenges[0] / jnp.sqrt(jnp.float32(total_rows))
    gamma = challenges[1]
    numer = 1.0 + step_size * (extended[0] + gamma * extended[1])
    denom = 1.0 + step_size * (extended[2] + gamma * extended[3])
    ratio_log = jnp.log(numer) - jnp.log(denom)
    own_terms = ratio_log[:rows_dev]
    running_sum = jnp.cumsum(own_terms)
    offset = entering(running_sum[-1], ("rows", "cols"), add_terms, jnp.float32(0.0))
    running = jnp.exp(offset + running_sum - own_terms)
    window = own_terms
    for shift_step in range(1, BLOWUP):
        window = window + ratio_log[shift_step : shift_step + rows_dev]
    grand = running * (jnp.exp(window) * denom[:rows_dev] - numer[:rows_dev]) / step_size
    picked = selectors.astype(jnp.float32)
    combined = (
        jnp.sum(alpha[:width, None] * picked[:width] * cons, axis=0)
        + alpha[width] * picked[width] * grand
    )
    quotient = divisor_inv * combined
    parts = rows_dev // devices
    gathered = regroup(quotient.reshape(1, rows_dev)).reshape(devices, parts)
    block_index = jnp.arange(devices, dtype=jnp.int32)
    cos_block, sin_block = turns(block_index[:, None] * block_index[None, :], devices, -1.0)
    first_re = jnp.dot(cos_block, gathered, precision=highest, preferred_element_type=jnp.float32)
    first_im = jnp.dot(sin_block, gathered, precision=highest, preferred_element_type=jnp.float32)
    global_pos = flat_index * parts + jnp.arange(parts, dtype=jnp.int32)
    twist_cos, twist_sin = turns(block_index[:, None] * global_pos[None, :], total_rows, -1.0)
    first_re, first_im = complex_mul(first_re, first_im, twist_cos, twist_sin)
    ordered = (
        jnp.stack([first_re, first_im])
        .reshape(2, n_cols, n_rows, parts)
        .transpose(0, 2, 1, 3)
        .reshape(2, devices * parts)
    )
    columns = regroup(ordered)
    coef_re, coef_im = local_dft(columns[0], columns[1], -1.0)
    coef_re = coef_re / total_rows
    coef_im = coef_im / total_rows
    seg_dev = SEGMENTS // n_cols
    seg_rows = rows_dev // SEGMENTS
    packed = jnp.stack([coef_re, coef_im]).reshape(2, n_cols, seg_dev, seg_rows)
    owned = column_relay(packed)
    owned = owned.transpose(0, 2, 3, 1).reshape(2, seg_dev, seg_rows * n_cols)
    short = seg_rows * n_cols
    band = short * SEGMENTS
    phase_index = jnp.arange(SEGMENTS, dtype=jnp.int32)
    short_index = jnp.arange(short, dtype=jnp.int32)
    phase_cos, phase_sin = turns(phase_index[:, None] * short_index[None, :], band, 1.0)
    spread_re, spread_im = complex_mul(
        owned[0][:, None, :], owned[1][:, None, :], phase_cos, phase_sin
    )
    lift_re, lift_im = local_dft(spread_re, spread_im, 1.0)
    lift_re = jnp.swapaxes(lift_re, 1, 2).reshape(seg_dev, band)
    lift_im = jnp.swapaxes(lift_im, 1, 2).reshape(seg_dev, band)
    band_index = jnp.arange(band, dtype=jnp.int32)
    shift_cos, shift_sin = turns(band_index * row_index, total_rows, 1.0)
    lift_re, lift_im = complex_mul(lift_re, lift_im, shift_cos, shift_sin)
    lifted = jnp.stack([lift_re, lift_im])
    slab = band // n_rows
    small = band // devices
    row_ids = jnp.arange(n_rows, dtype=jnp.int32)
    cos_rows, sin_rows = turns(row_ids[:, None] * row_ids[None, :], n_rows, 1.0)
    pieces = lifted.reshape(2, seg_dev, n_rows, slab).transpose(0, 2, 1, 3)
    arrived = lax.all_to_all(pieces, "rows", split_axis=1, concat_axis=1, tiled=True)
    summed_re = jnp.einsum("ab,b...->a...", cos_rows, arrived[0], precision=highest) - jnp.einsum(
        "ab,b...->a...", sin_rows, arrived[1], precision=highest
    )
    summed_im = jnp.einsum("ab,b...->a...", sin_rows, arrived[0], precision=highest) + jnp.einsum(
        "ab,b...->a...", cos_rows, arrived[1], precision=highest
    )
    outgoing = (
        jnp.stack([summed_re, summed_im])
        .reshape(2, n_rows, seg_dev, n_cols, small)
        .transpose(0, 3, 2, 1, 4)
    )
    landed = column_relay(outgoing)
    values = landed.reshape(2, SEGMENTS, n_rows, small)
    leaf_count = n_rows * small
    real_part = values[0].reshape(SEGMENTS, leaf_count)
    imag_part = values[1].reshape(SEGMENTS, leaf_count)
    zeros = jnp.zeros((DIGEST, leaf_count), jnp.float32)
    state = permute(jnp.concatenate([zeros, real_part], axis=0), hash_mds, hash_rc)
    state = state + jnp.concatenate([zeros, imag_part], axis=0)
    state = permute(state, hash_mds, hash_rc)
    return state[:DIGEST].reshape(DIGEST, n_rows, small)


def solution(mesh):
    in_specs = (
        P(None, ("rows", "cols")),
        P(None, ("rows", "cols")),
        P(),
        P(),
        P(),
        P(),
        P(("rows", "cols")),
        P(),
        P(),
    )
    out_specs = P(None, None, ("rows", "cols"))
    return jax.shard_map(
        on_device, mesh=mesh, in_specs=in_specs, out_specs=out_specs, check_vma=False
    )
```

profile of v0, /device:TPU:1, one launch (start us, length us, event | category | flops | bytes accessed | tf_op | source)
XLA Modules:
  0.0 759.6 jit_solution(3835214216266359357)
XLA Ops:
  2.1 7.3 constant_dynamic-update-slice_fusion.1
  21.2 5.7 log_subtract_fusion
  32.2 70.3 %all-reduce.3 = f32[128]{0:T(128)S(1)} all-reduce(f32[128]{0:T(128)S(1)} %slice_dynamic-update-slice_fusion), channel_id=1, replica_groups=mesh['rows'=16,'cols'=8] {'rows','cols'}, use_global_device_ids=true, to_apply=%add.3 | all-reduce | flops 128 | bytes 1024
  102.5 159.7 %while.13 = (s32[]{:T(128)}, f32[]{:T(128)}, s32[]{:T(128)}, f32[128]{0:T(128)S(1)}, s32[]{:T(128)}) while((s32[]{:T(128)}, f32[]{:T(128)}, s32[]{:T(128)}, f32[128]{0:T(128)S(1)}, s32[]{:T(128)}) %tuple.45), condition=%wide.region_5.6_spmd, body=%wide.region_4.5_spmd.sunk | while | flops 5 | bytes 115 | solution.py:31
  262.3 15.9 %fusion.7 = f32[65536]{0:T(1024)S(1)} fusion(f32[32,65536]{1,0:T(8,128)} %param.11, f32[32,65544]{1,0:T(8,128)} %constant_dynamic-update-slice_fusion, f32[33,65536]{1,0:T(8,128)} %copy-done.2, f32[32]{0:T(128)S(1)} %copy-done.10, f32[32]{0:T(128)S(1)} %bitcast.216, f32[32,32]{1,0:T(8,128)S(1)} %copy-done), kind=kOutput, calls=%fused_computation.14 | convolution fusion | flops 819920896 | bytes 33820928 | tf_op jit(solution)/shard_map/dot_general | solution.py:110
  283.8 10.8 %all-to-all-done = f32[1,128,512]{2,0,1:T(1,128)S(1)} async-done(((f32[1,128,512]{2,0,1:T(1,128)}), f32[1,128,512]{2,0,1:T(1,128)S(1)}, u32[]{:S(2)}, u32[]{:S(2)}) %all-to-all-start) | async-done | bytes 262176 | tf_op jit(solution)/shard_map/all_to_all | solution.py:87
  297.6 18.1 %all_to_all.33 = f32[2,128,512]{2,0,1:T(2,128)S(1)} all-to-all(f32[2,128,512]{2,0,1:T(2,128)S(1)} %copy.39), channel_id=1, replica_groups=mesh['rows'=16,'cols'=8] {'rows','cols'}, dimensions={1} | all-to-all | bytes 1048576 | tf_op jit(solution)/shard_map/all_to_all | solution.py:87
  318.7 5.8 fusion.80
  324.5 6.0 fusion.79
  330.5 5.8 fusion.56
  336.4 6.2 fusion.57
  350.8 7.2 all-to-all-done.2
  372.1 9.4 %fusion.71 = f32[8,512,128]{2,1,0:T(8,128)S(1)} fusion(f32[128,512]{0,1:T(8,128)S(1)} %copy.44, s32[128,512]{0,1:T(8,128)S(1)} %multiply_add_fusion.6, f32[128,512]{0,1:T(8,128)S(1)} %copy.42), kind=kOutput, calls=%fused_computation.108 | convolution fusion | flops 814448640 | bytes 2883584 | tf_op jit(solution)/shard_map/kn,...nm->...km/dot_general | solution.py:69
  381.4 9.5 %fusion.70 = f32[8,512,128]{2,1,0:T(8,128)S(1)} fusion(f32[128,512]{0,1:T(8,128)S(1)} %copy.44, s32[128,512]{0,1:T(8,128)S(1)} %multiply_add_fusion.6, f32[128,512]{0,1:T(8,128)S(1)} %copy.42), kind=kOutput, calls=%fused_computation.107 | convolution fusion | flops 814448640 | bytes 2883584 | tf_op jit(solution)/shard_map/kn,...nm->...km/dot_general | solution.py:66
  391.0 9.7 %convolution_add_fusion.5 = f32[8,512,128]{2,1,0:T(8,128)S(1)} fusion(f32[8,512,128]{2,1,0:T(8,128)S(1)} %fusion.71, f32[128,512]{0,1:T(8,128)S(1)} %copy.44, s32[128,512]{0,1:T(8,128)S(1)} %multiply_add_fusion.6, f32[128,512]{0,1:T(8,128)S(1)} %copy.42), kind=kOutput, calls=%fused_computation.83 | convolution fusion | flops 814972928 | bytes 4980736 | tf_op jit(solution)/shard_map/kn,...nm->...km/dot_general | solution.py:69
  400.7 9.6 %convolution_subtract_fusion.1 = f32[8,512,128]{2,1,0:T(8,128)S(1)} fusion(f32[8,512,128]{2,1,0:T(8,128)S(1)} %fusion.70, f32[128,512]{0,1:T(8,128)S(1)} %copy.44, s32[128,512]{0,1:T(8,128)S(1)} %multiply_add_fusion.6, f32[128,512]{0,1:T(8,128)S(1)} %copy.42), kind=kOutput, calls=%fused_computation.84 | convolution fusion | flops 814972928 | bytes 4980736 | tf_op jit(solution)/shard_map/kn,...nm->...km/dot_general | solution.py:66
  410.3 10.9 %fusion.62 = f32[8,128,512]{2,1,0:T(8,128)S(1)} fusion(f32[8,512,128]{2,1,0:T(8,128)S(1)} %convolution_add_fusion.5, f32[8,512,128]{2,1,0:T(8,128)S(1)} %convolution_subtract_fusion.1, f32[128,512]{0,1:T(8,128)S(1)} %copy.46, f32[128,512]{0,1:T(8,128)S(1)} %copy.45), kind=kOutput, calls=%fused_computation.99 | convolution fusion | flops 3226468352 | bytes 6815744 | tf_op jit(solution)/shard_map/...kn,jn->...kj/dot_general | solution.py:78
  421.2 12.2 %fusion.66 = f32[8,128,512]{2,1,0:T(8,128)} fusion(f32[8,512,128]{2,1,0:T(8,128)S(1)} %convolution_add_fusion.5, f32[8,512,128]{2,1,0:T(8,128)S(1)} %convolution_subtract_fusion.1, f32[128,512]{0,1:T(8,128)S(1)} %copy.46, f32[128,512]{0,1:T(8,128)S(1)} %copy.45), kind=kOutput, calls=%fused_computation.103 | convolution fusion | flops 3226468352 | bytes 6815744 | tf_op jit(solution)/shard_map/...kn,jn->...kj/dot_general | solution.py:75
  433.3 11.8 %add_bitcast_fusion = f32[1,8,512,128]{2,3,1,0:T(8,128)} fusion(f32[8,128,512]{2,1,0:T(8,128)S(1)} %fusion.62, f32[8,512,128]{2,1,0:T(8,128)S(1)} %convolution_add_fusion.5, f32[8,512,128]{2,1,0:T(8,128)S(1)} %convolution_subtract_fusion.1, f32[128,512]{0,1:T(8,128)S(1)} %copy.46, f32[128,512]{0,1:T(8,128)S(1)} %copy.45), kind=kOutput, calls=%fused_computation.72 | convolution fusion | flops 3226992640 | bytes 8912896 | tf_op jit(solution)/shard_map/...kn,jn->...kj/dot_general | solution.py:78
  448.0 13.7 %subtract_bitcast_fusion = f32[1,8,512,128]{2,3,1,0:T(8,128)} fusion(f32[8,128,512]{2,1,0:T(8,128)} %fusion.66, f32[8,512,128]{2,1,0:T(8,128)S(1)} %convolution_add_fusion.5, f32[8,512,128]{2,1,0:T(8,128)} %copy-done.3, f32[128,512]{0,1:T(8,128)S(1)} %copy.46, f32[128,512]{0,1:T(8,128)S(1)} %copy.45), kind=kOutput, calls=%fused_computation.73 | convolution fusion | flops 3226992640 | bytes 8912896 | tf_op jit(solution)/shard_map/...kn,jn->...kj/dot_general | solution.py:75
  463.6 16.3 %copy.50 = f32[1,65536,8]{2,1,0:T(8,128)} copy(f32[1,65536,8]{1,0,2:T(1,128)S(1)} %bitcast.193) | data formatting | bytes 4194304 | tf_op jit(solution)/shard_map/transpose | solution.py:164
  479.9 45.5 %reshape.484 = f32[1,16,1,32768]{3,1,2,0:T(8,128)} reshape(f32[1,65536,8]{2,1,0:T(8,128)} %copy.50) | data formatting | bytes 4194304 | tf_op jit(solution)/shard_map/reshape | solution.py:164
  525.4 16.3 %copy.54 = f32[1,65536,8]{2,1,0:T(8,128)} copy(f32[1,65536,8]{1,0,2:T(1,128)S(1)} %bitcast.190) | data formatting | bytes 4194304 | tf_op jit(solution)/shard_map/transpose | solution.py:165
  541.7 45.6 %reshape.486 = f32[1,16,1,32768]{3,1,2,0:T(8,128)} reshape(f32[1,65536,8]{2,1,0:T(8,128)} %copy.54) | data formatting | bytes 4194304 | tf_op jit(solution)/shard_map/reshape | solution.py:165
  587.3 9.9 %multiply_subtract_fusion = (f32[1,16,1,32768]{3,1,2,0:T(8,128)S(1)}, f32[1,16,1,32768]{3,1,2,0:T(8,128)S(1)}) fusion(f32[1,16,1,32768]{3,1,2,0:T(8,128)} %reshape.486, f32[1,16,1,32768]{3,1,2,0:T(8,128)S(1)} %copy-done.5, s32[]{:T(128)S(6)} %axis_index.17), kind=kLoop, calls=%fused_computation.71 | loop fusion | flops 11534336 | bytes 8388612 | tf_op jit(solution)/shard_map/sub | solution.py:53
  597.4 6.3 copy.55
  603.7 52.9 %all_to_all.34 = f32[2,16,1,32768]{3,2,0,1:T(1,128)S(1)} all-to-all(f32[2,16,1,32768]{3,2,0,1:T(1,128)} %copy.55), channel_id=1, replica_groups=mesh['rows'=16,'cols'=8] {'rows'}, dimensions={1} | all-to-all | bytes 8388608 | tf_op jit(solution)/shard_map/all_to_all | solution.py:175
  676.0 7.0 all-to-all-start.4
  683.0 48.8 %all-to-all-done.4 = f32[2,8,1,16,4096]{4,3,2,0,1:T(8,128)} async-done(((f32[2,8,1,16,4096]{4,3,2,0,1:T(8,128)}), f32[2,8,1,16,4096]{4,3,2,0,1:T(8,128)}, u32[]{:S(2)}, u32[]{:S(2)}) %all-to-all-start.4) | async-done | bytes 4194336 | tf_op jit(solution)/shard_map/all_to_all | solution.py:91
  736.8 5.3 fusion.4
  742.1 5.6 fusion.3
  747.7 5.0 fusion.1
  (226 shorter events, 164.6 us)
Async XLA Ops:
  0.0 262.3 %copy-start = (f32[32,32]{1,0:T(8,128)S(1)}, f32[32,32]{1,0:T(8,128)}, u32[]{:S(2)}) copy-start(f32[32,32]{1,0:T(8,128)} %param.13) | copy-start | bytes 12292
  0.7 19.8 %collective-permute-start = (f32[32,8]{1,0:T(8,128)S(1)}, f32[32,8]{1,0:T(8,128)S(1)}, u32[]{:S(2)}, u32[]{:S(2)}) collective-permute-start(f32[32,8]{1,0:T(8,128)S(1)} %slice.133), channel_id=1, source_target_pairs={{0,127},{1,0},{2,1},{3,2},{4,3},{5,4},{6,5},{7,6},{8,7},{9,8},{10,... | collective-permute-start | bytes 3080 | tf_op jit(solution)/shard_map/ppermute | solution.py:19
  2.1 7.3 copy-start.11
  2.1 7.9 %copy-start.8 = (f32[2]{0:T(128)S(1)}, f32[2]{0:T(128)}, u32[]{:S(2)}) copy-start(f32[2]{0:T(128)} %param.16) | copy-start | bytes 28
  15.2 4.0 copy-start.2
  30.8 231.5 %copy-start.10 = (f32[32]{0:T(128)S(1)}, f32[32]{0:T(128)}, u32[]{:S(2)}) copy-start(f32[32]{0:T(128)} %param.14) | copy-start | bytes 388
  262.3 15.9 %copy-start.6 = (f32[65536]{0:T(1024)S(1)}, f32[65536]{0:T(1024)}, u32[]{:S(2)}) copy-start(f32[65536]{0:T(1024)} %param.17) | copy-start | bytes 786436
  279.1 15.5 %all-to-all-start = ((f32[1,128,512]{2,0,1:T(1,128)}), f32[1,128,512]{2,0,1:T(1,128)S(1)}, u32[]{:S(2)}, u32[]{:S(2)}) async-start(f32[1,128,512]{2,0,1:T(1,128)} %bitcast.19), calls=%async_computation | async-start | bytes 524288 | tf_op jit(solution)/shard_map/all_to_all | solution.py:87
  343.9 14.0 %all-to-all-start.2 = ((f32[2,8,1,8192]{3,0,2,1:T(2,128)}), f32[2,8,1,8192]{3,0,2,1:T(2,128)S(1)}, u32[]{:S(2)}, u32[]{:S(2)}) async-start(f32[2,8,1,8192]{3,0,2,1:T(2,128)} %copy.40), calls=%async_computation.2 | async-start | bytes 1048576 | tf_op jit(solution)/shard_map/all_to_all | solution.py:91
  410.3 23.0 %copy-start.3 = (f32[8,512,128]{2,1,0:T(8,128)}, f32[8,512,128]{2,1,0:T(8,128)S(1)}, u32[]{:S(2)}) copy-start(f32[8,512,128]{2,1,0:T(8,128)S(1)} %convolution_subtract_fusion.1) | copy-start | bytes 6291460
  479.9 45.5 %copy-start.4 = (f32[1,8,512,128]{3,2,0,1:T(8,128)S(1)}, f32[1,8,512,128]{3,2,0,1:T(8,128)}, u32[]{:S(2)}) copy-start(f32[1,8,512,128]{3,2,0,1:T(8,128)} %copy.53) | copy-start | bytes 6291460
  541.7 45.6 %copy-start.5 = (f32[1,16,1,32768]{3,1,2,0:T(8,128)S(1)}, f32[1,16,1,32768]{3,1,2,0:T(8,128)}, u32[]{:S(2)}) copy-start(f32[1,16,1,32768]{3,1,2,0:T(8,128)} %reshape.484) | copy-start | bytes 6291460
  676.0 7.0 copy-start.9
  676.0 55.8 %all-to-all-start.4 = ((f32[2,8,1,16,4096]{4,3,2,0,1:T(8,128)}), f32[2,8,1,16,4096]{4,3,2,0,1:T(8,128)}, u32[]{:S(2)}, u32[]{:S(2)}) async-start(f32[2,8,1,16,4096]{4,3,2,0,1:T(8,128)} %maximum_bitcast_fusion), calls=%async_computation.4 | async-start | bytes 8388608 | tf_op jit(solution)/shard_map/all_to_all | solution.py:91
  735.6 1.2 copy-start.7
  752.7 6.7 copy-start.1
where the time goes:
time: 770 us; the launch traced here: 760 us
  local copies, waits for them, and re-layouts  258 us (34%)
  matrix products  164 us (21%)
  blocking collectives  141 us (18%)
  loops' own time  83.6 us (11%)
  waiting for transfers between devices  66.7 us (9%)
  other arithmetic  27.1 us (4%)
  starting transfers between devices  17.7 us (2%)
    another operation x1, loops' own time, entering(): return lax.fori_loop(0, count - 1, turn, subtotal)  83.6 us
    dynamic_slice x127, local copies, waits for them, and re-layouts, turn(): longer = join(subtotal, pieces[position])  76.1 us
    unnamed x1, blocking collectives  70.3 us
    all_to_all x2, waiting for transfers between devices, column_relay(): lax.all_to_all(values, 'cols', split_axis=1, concat_axis=1, tiled=True)  56 us
    all_to_all x1, blocking collectives, on_device(): lax.all_to_all(pieces, 'rows', split_axis=1, concat_axis=1, tiled=True)  52.9 us
    reshape x1, local copies, waits for them, and re-layouts, on_device(): lift_im = jnp.swapaxes(lift_im, 1, 2).reshape(seg_dev, band)  45.6 us
    reshape x1, local copies, waits for them, and re-layouts, on_device(): lift_re = jnp.swapaxes(lift_re, 1, 2).reshape(seg_dev, band)  45.5 us
    dot_general x4, matrix products, permute(): jnp.dot(hash_mds, squash(state), precision=highest, preferred_element_typ...  20.8 us
  transfers between devices with their start and end apart: 4, of which 3 were waited for; matrix products, arithmetic and copies ran while one was open for 2% of the time, Pallas kernels for 0%

commit v1 on v0

--- a/solution.py
+++ b/solution.py
@@ -19,16 +19,12 @@
     return lax.ppermute(array, axis, [(i, (i + by) % count) for i in range(count)])
 
 
-def entering(value, axis, join, neutral):
+def entering(value, axis):
     count, mine = (lax.axis_size(axis), lax.axis_index(axis))
-    pieces = lax.all_gather(value, axis)
-    subtotal = jnp.full_like(value, 0) + jnp.asarray(neutral, value.dtype)
-
-    def turn(position, subtotal):
-        longer = join(subtotal, pieces[position])
-        return jnp.where(position < mine, longer, subtotal)
-
-    return lax.fori_loop(0, count - 1, turn, subtotal)
+    spread = jnp.broadcast_to(value, (count,))
+    pieces = lax.all_to_all(spread, axis, 0, 0, tiled=True)
+    earlier = jnp.arange(count, dtype=jnp.int32) < mine
+    return jnp.sum(jnp.where(earlier, pieces, jnp.zeros_like(pieces)))
 
 
 def squash(value):
@@ -89,10 +85,6 @@
 
 def column_relay(values):
     return lax.all_to_all(values, "cols", split_axis=1, concat_axis=1, tiled=True)
-
-
-def add_terms(earlier, later):
-    return earlier + later
 
 
 def on_device(trace, selectors, mds, quad, alpha, challenges, divisor_inv, hash_mds, hash_rc):
@@ -116,7 +108,7 @@
     ratio_log = jnp.log(numer) - jnp.log(denom)
     own_terms = ratio_log[:rows_dev]
     running_sum = jnp.cumsum(own_terms)
-    offset = entering(running_sum[-1], ("rows", "cols"), add_terms, jnp.float32(0.0))
+    offset = entering(running_sum[-1], ("rows", "cols"))
     running = jnp.exp(offset + running_sum - own_terms)
     window = own_terms
     for shift_step in range(1, BLOWUP):

time: 770 us -> 561 us (0.73)
  loops' own time: 83.6 us -> 0 us
  local copies, waits for them, and re-layouts: 258 us -> 185 us
  blocking collectives: 141 us -> 71 us
  starting transfers between devices: 17.7 us -> 35.1 us
    another operation x1 -> x0, loops' own time: 83.6 us -> none  [entering(): return lax.fori_loop(0, count - 1, turn, subtotal)]
    dynamic_slice x127 -> x0, local copies, waits for them, and re-layouts: 76.1 us -> none  [turn(): longer = join(subtotal, pieces[position])]
    unnamed x1 -> x0, blocking collectives: 70.3 us -> none
    all_to_all x0 -> x1, starting transfers between devices: none -> 12.2 us  [entering(): pieces = lax.all_to_all(spread, axis, 0, 0, tiled=True)]
    unnamed x33 -> x29, local copies, waits for them, and re-layouts: 20.6 us -> 20.4 us
  transfers between devices with their start and end apart: 4 -> 5, of which waited for: 3 -> 3; matrix products, arithmetic and copies ran while one was open for 2% -> 6% of each run, Pallas kernels for 0% -> 0%
where the time goes in v1:
time: 561 us; the launch traced here: 554 us
  local copies, waits for them, and re-layouts  185 us (33%)
  matrix products  164 us (29%)
  blocking collectives  71 us (13%)
  waiting for transfers between devices  66.7 us (12%)
  starting transfers between devices  35.1 us (6%)
  other arithmetic  31.1 us (6%)
    all_to_all x2, waiting for transfers between devices, column_relay(): lax.all_to_all(values, 'cols', split_axis=1, concat_axis=1, tiled=True)  56 us
    all_to_all x1, blocking collectives, on_device(): lax.all_to_all(pieces, 'rows', split_axis=1, concat_axis=1, tiled=True)  53 us
    reshape x1, local copies, waits for them, and re-layouts, on_device(): lift_im = jnp.swapaxes(lift_im, 1, 2).reshape(seg_dev, band)  45.6 us
    reshape x1, local copies, waits for them, and re-layouts, on_device(): lift_re = jnp.swapaxes(lift_re, 1, 2).reshape(seg_dev, band)  45.5 us
    dot_general x4, matrix products, permute(): jnp.dot(hash_mds, squash(state), precision=highest, preferred_element_typ...  20.8 us
    unnamed x29, local copies, waits for them, and re-layouts  20.4 us
    dot_general x2, matrix products, local_dft(): jnp.einsum('...kn,jn->...kj', section_im, sin_two, precision=highest)  19.9 us
    dot_general x2, matrix products, local_dft(): jnp.einsum('...kn,jn->...kj', section_re, cos_two, precision=highest)  18.2 us
  transfers between devices with their start and end apart: 5, of which 3 were waited for; matrix products, arithmetic and copies ran while one was open for 6% of the time, Pallas kernels for 0%

profile of v1, /device:TPU:1, one launch (start us, length us, event | category | flops | bytes accessed | tf_op | source)
XLA Modules:
  0.0 554.4 jit_solution(12262380253753366624)
XLA Ops:
  2.1 7.3 %constant_dynamic-update-slice_fusion.1 = f32[32,65544]{1,0:T(8,128)} fusion(f32[32,65536]{1,0:T(8,128)} %param.9), kind=kLoop, calls=%fused_computation.222 | loop fusion | bytes 16777216
  21.3 5.5 %log_subtract_fusion = (f32[1,65544]{1,0:T(1,128)S(1)}, f32[1,65544]{1,0:T(1,128)S(1)}, f32[1,65544]{1,0:T(1,128)S(1)}) fusion(f32[32,65544]{1,0:T(8,128)} %constant_dynamic-update-slice_fusion, f32[]{:T(128)} %bitcast.3, f32[]{:T(128)} %bitcast.2), kind=kLoop, calls=%fused_computation.142 | loop fusion | flops 589896 | bytes 1835240 | tf_op jit(solution)/shard_map/sub | solution.py:108
  35.5 12.2 %all-to-all-start = ((f32[128,1,1]{2,1,0:T(1,128)}), f32[128,1,1]{2,1,0:T(1,128)S(1)}, u32[]{:S(2)}, u32[]{:S(2)}) async-start(f32[128,1,1]{2,1,0:T(1,128)} %broadcast_in_dim.4), calls=%async_computation | async-start | bytes 131072 | tf_op jit(solution)/shard_map/all_to_all | solution.py:25
  47.7 15.9 %fusion.7 = f32[65536]{0:T(1024)S(1)} fusion(f32[32,65536]{1,0:T(8,128)} %param.9, f32[32,65544]{1,0:T(8,128)} %constant_dynamic-update-slice_fusion, f32[33,65536]{1,0:T(8,128)} %copy-done.2, f32[32]{0:T(128)S(1)} %copy-done.9, f32[32]{0:T(128)S(1)} %bitcast.214, f32[32,32]{1,0:T(8,128)S(1)} %copy-done), kind=kOutput, calls=%fused_computation.14 | convolution fusion | flops 819920896 | bytes 33820928 | tf_op jit(solution)/shard_map/dot_general | solution.py:102
  68.6 9.9 %all-to-all-start.1 = ((f32[1,128,512]{2,0,1:T(1,128)}), f32[1,128,512]{2,0,1:T(1,128)S(1)}, u32[]{:S(2)}, u32[]{:S(2)}) async-start(f32[1,128,512]{2,0,1:T(1,128)} %bitcast.19), calls=%async_computation.1 | async-start | bytes 524288 | tf_op jit(solution)/shard_map/all_to_all | solution.py:83
  78.6 10.8 %all-to-all-done.1 = f32[1,128,512]{2,0,1:T(1,128)S(1)} async-done(((f32[1,128,512]{2,0,1:T(1,128)}), f32[1,128,512]{2,0,1:T(1,128)S(1)}, u32[]{:S(2)}, u32[]{:S(2)}) %all-to-all-start.1) | async-done | bytes 262176 | tf_op jit(solution)/shard_map/all_to_all | solution.py:83
  92.4 18.1 %all_to_all.42 = f32[2,128,512]{2,0,1:T(2,128)S(1)} all-to-all(f32[2,128,512]{2,0,1:T(2,128)S(1)} %copy.62), channel_id=1, replica_groups=mesh['rows'=16,'cols'=8] {'rows','cols'}, dimensions={1} | all-to-all | bytes 1048576 | tf_op jit(solution)/shard_map/all_to_all | solution.py:83
  113.5 5.8 %fusion.80 = f32[512,128]{1,0:T(8,128)S(1)} fusion(f32[128,512]{1,0:T(8,128)S(1)} %convolution_add_fusion.6, f32[128,512]{1,0:T(8,128)S(1)} %convolution_subtract_fusion.2), kind=kOutput, calls=%fused_computation.121 | convolution fusion | flops 407437312 | bytes 786432 | tf_op jit(solution)/shard_map/...kn,jn->...kj/dot_general | solution.py:74
  119.3 6.0 %fusion.79 = f32[512,128]{1,0:T(8,128)S(1)} fusion(f32[128,512]{1,0:T(8,128)S(1)} %convolution_add_fusion.6, f32[128,512]{1,0:T(8,128)S(1)} %convolution_subtract_fusion.2), kind=kOutput, calls=%fused_computation.120 | convolution fusion | flops 407437312 | bytes 786432 | tf_op jit(solution)/shard_map/...kn,jn->...kj/dot_general | solution.py:71
  125.3 5.8 %fusion.56 = f32[512,128]{1,0:T(8,128)S(1)} fusion(f32[512,128]{1,0:T(8,128)S(1)} %fusion.80, f32[128,512]{1,0:T(8,128)S(1)} %convolution_add_fusion.6, f32[128,512]{1,0:T(8,128)S(1)} %convolution_subtract_fusion.2), kind=kOutput, calls=%fused_computation.91 | convolution fusion | flops 407568384 | bytes 1048576 | tf_op jit(solution)/shard_map/...kn,jn->...kj/dot_general | solution.py:74
  131.2 6.2 %fusion.57 = f32[512,128]{1,0:T(8,128)S(1)} fusion(f32[512,128]{1,0:T(8,128)S(1)} %fusion.79, f32[128,512]{1,0:T(8,128)S(1)} %convolution_add_fusion.6, f32[128,512]{1,0:T(8,128)S(1)} %convolution_subtract_fusion.2), kind=kOutput, calls=%fused_computation.93 | convolution fusion | flops 407568384 | bytes 1048576 | tf_op jit(solution)/shard_map/...kn,jn->...kj/dot_general | solution.py:71
  145.6 7.2 %all-to-all-done.3 = f32[2,8,1,8192]{3,0,2,1:T(2,128)S(1)} async-done(((f32[2,8,1,8192]{3,0,2,1:T(2,128)}), f32[2,8,1,8192]{3,0,2,1:T(2,128)S(1)}, u32[]{:S(2)}, u32[]{:S(2)}) %all-to-all-start.3) | async-done | bytes 524320 | tf_op jit(solution)/shard_map/all_to_all | solution.py:87
  166.8 9.4 %fusion.71 = f32[8,512,128]{2,1,0:T(8,128)S(1)} fusion(f32[128,512]{0,1:T(8,128)S(1)} %copy.67, s32[128,512]{0,1:T(8,128)S(1)} %multiply_add_fusion.6, f32[128,512]{0,1:T(8,128)S(1)} %copy.65), kind=kOutput, calls=%fused_computation.108 | convolution fusion | flops 814448640 | bytes 2883584 | tf_op jit(solution)/shard_map/kn,...nm->...km/dot_general | solution.py:65
  176.2 9.5 %fusion.70 = f32[8,512,128]{2,1,0:T(8,128)S(1)} fusion(f32[128,512]{0,1:T(8,128)S(1)} %copy.67, s32[128,512]{0,1:T(8,128)S(1)} %multiply_add_fusion.6, f32[128,512]{0,1:T(8,128)S(1)} %copy.65), kind=kOutput, calls=%fused_computation.107 | convolution fusion | flops 814448640 | bytes 2883584 | tf_op jit(solution)/shard_map/kn,...nm->...km/dot_general | solution.py:62
  185.7 9.7 %convolution_add_fusion.5 = f32[8,512,128]{2,1,0:T(8,128)S(1)} fusion(f32[8,512,128]{2,1,0:T(8,128)S(1)} %fusion.71, f32[128,512]{0,1:T(8,128)S(1)} %copy.67, s32[128,512]{0,1:T(8,128)S(1)} %multiply_add_fusion.6, f32[128,512]{0,1:T(8,128)S(1)} %copy.65), kind=kOutput, calls=%fused_computation.83 | convolution fusion | flops 814972928 | bytes 4980736 | tf_op jit(solution)/shard_map/kn,...nm->...km/dot_general | solution.py:65
  195.5 9.6 %convolution_subtract_fusion.1 = f32[8,512,128]{2,1,0:T(8,128)S(1)} fusion(f32[8,512,128]{2,1,0:T(8,128)S(1)} %fusion.70, f32[128,512]{0,1:T(8,128)S(1)} %copy.67, s32[128,512]{0,1:T(8,128)S(1)} %multiply_add_fusion.6, f32[128,512]{0,1:T(8,128)S(1)} %copy.65), kind=kOutput, calls=%fused_computation.84 | convolution fusion | flops 814972928 | bytes 4980736 | tf_op jit(solution)/shard_map/kn,...nm->...km/dot_general | solution.py:62
  205.1 10.9 %fusion.62 = f32[8,128,512]{2,1,0:T(8,128)S(1)} fusion(f32[8,512,128]{2,1,0:T(8,128)S(1)} %convolution_add_fusion.5, f32[8,512,128]{2,1,0:T(8,128)S(1)} %convolution_subtract_fusion.1, f32[128,512]{0,1:T(8,128)S(1)} %copy.69, f32[128,512]{0,1:T(8,128)S(1)} %copy.68), kind=kOutput, calls=%fused_computation.99 | convolution fusion | flops 3226468352 | bytes 6815744 | tf_op jit(solution)/shard_map/...kn,jn->...kj/dot_general | solution.py:74
  215.9 12.2 %fusion.66 = f32[8,128,512]{2,1,0:T(8,128)} fusion(f32[8,512,128]{2,1,0:T(8,128)S(1)} %convolution_add_fusion.5, f32[8,512,128]{2,1,0:T(8,128)S(1)} %convolution_subtract_fusion.1, f32[128,512]{0,1:T(8,128)S(1)} %copy.69, f32[128,512]{0,1:T(8,128)S(1)} %copy.68), kind=kOutput, calls=%fused_computation.103 | convolution fusion | flops 3226468352 | bytes 6815744 | tf_op jit(solution)/shard_map/...kn,jn->...kj/dot_general | solution.py:71
  228.1 11.8 %add_bitcast_fusion = f32[1,8,512,128]{2,3,1,0:T(8,128)} fusion(f32[8,128,512]{2,1,0:T(8,128)S(1)} %fusion.62, f32[8,512,128]{2,1,0:T(8,128)S(1)} %convolution_add_fusion.5, f32[8,512,128]{2,1,0:T(8,128)S(1)} %convolution_subtract_fusion.1, f32[128,512]{0,1:T(8,128)S(1)} %copy.69, f32[128,512]{0,1:T(8,128)S(1)} %copy.68), kind=kOutput, calls=%fused_computation.72 | convolution fusion | flops 3226992640 | bytes 8912896 | tf_op jit(solution)/shard_map/...kn,jn->...kj/dot_general | solution.py:74
  242.8 13.7 %subtract_bitcast_fusion = f32[1,8,512,128]{2,3,1,0:T(8,128)} fusion(f32[8,128,512]{2,1,0:T(8,128)} %fusion.66, f32[8,512,128]{2,1,0:T(8,128)S(1)} %convolution_add_fusion.5, f32[8,512,128]{2,1,0:T(8,128)} %copy-done.3, f32[128,512]{0,1:T(8,128)S(1)} %copy.69, f32[128,512]{0,1:T(8,128)S(1)} %copy.68), kind=kOutput, calls=%fused_computation.73 | convolution fusion | flops 3226992640 | bytes 8912896 | tf_op jit(solution)/shard_map/...kn,jn->...kj/dot_general | solution.py:71
  258.4 16.3 %copy.73 = f32[1,65536,8]{2,1,0:T(8,128)} copy(f32[1,65536,8]{1,0,2:T(1,128)S(1)} %bitcast.191) | data formatting | bytes 4194304 | tf_op jit(solution)/shard_map/transpose | solution.py:156
  274.7 45.5 %reshape.486 = f32[1,16,1,32768]{3,1,2,0:T(8,128)} reshape(f32[1,65536,8]{2,1,0:T(8,128)} %copy.73) | data formatting | bytes 4194304 | tf_op jit(solution)/shard_map/reshape | solution.py:156
  320.2 16.3 %copy.77 = f32[1,65536,8]{2,1,0:T(8,128)} copy(f32[1,65536,8]{1,0,2:T(1,128)S(1)} %bitcast.188) | data formatting | bytes 4194304 | tf_op jit(solution)/shard_map/transpose | solution.py:157
  336.5 45.6 %reshape.488 = f32[1,16,1,32768]{3,1,2,0:T(8,128)} reshape(f32[1,65536,8]{2,1,0:T(8,128)} %copy.77) | data formatting | bytes 4194304 | tf_op jit(solution)/shard_map/reshape | solution.py:157
  382.1 9.9 %multiply_subtract_fusion = (f32[1,16,1,32768]{3,1,2,0:T(8,128)S(1)}, f32[1,16,1,32768]{3,1,2,0:T(8,128)S(1)}) fusion(f32[1,16,1,32768]{3,1,2,0:T(8,128)} %reshape.488, f32[1,16,1,32768]{3,1,2,0:T(8,128)S(1)} %copy-done.5, s32[]{:T(128)S(6)} %axis_index.17), kind=kLoop, calls=%fused_computation.71 | loop fusion | flops 11534336 | bytes 8388612 | tf_op jit(solution)/shard_map/sub | solution.py:49
  392.3 6.3 %copy.78 = f32[2,16,1,32768]{3,2,0,1:T(1,128)} copy(f32[2,16,1,32768]{3,1,2,0:T(8,128)S(1)} %pad_maximum_fusion) | data formatting | bytes 8388608 | tf_op jit(solution)/shard_map/stack | solution.py:161
  398.5 53.0 %all_to_all.43 = f32[2,16,1,32768]{3,2,0,1:T(1,128)S(1)} all-to-all(f32[2,16,1,32768]{3,2,0,1:T(1,128)} %copy.78), channel_id=1, replica_groups=mesh['rows'=16,'cols'=8] {'rows'}, dimensions={1} | all-to-all | bytes 8388608 | tf_op jit(solution)/shard_map/all_to_all | solution.py:167
  470.8 7.0 %all-to-all-start.5 = ((f32[2,8,1,16,4096]{4,3,2,0,1:T(8,128)}), f32[2,8,1,16,4096]{4,3,2,0,1:T(8,128)}, u32[]{:S(2)}, u32[]{:S(2)}) async-start(f32[2,8,1,16,4096]{4,3,2,0,1:T(8,128)} %maximum_bitcast_fusion), calls=%async_computation.5 | async-start | bytes 8388608 | tf_op jit(solution)/shard_map/all_to_all | solution.py:87
  477.8 48.8 %all-to-all-done.5 = f32[2,8,1,16,4096]{4,3,2,0,1:T(8,128)} async-done(((f32[2,8,1,16,4096]{4,3,2,0,1:T(8,128)}), f32[2,8,1,16,4096]{4,3,2,0,1:T(8,128)}, u32[]{:S(2)}, u32[]{:S(2)}) %all-to-all-start.5) | async-done | bytes 4194336 | tf_op jit(solution)/shard_map/all_to_all | solution.py:87
  531.6 5.3 fusion.4
  536.9 5.6 %fusion.3 = f32[12,65536]{1,0:T(8,128)S(1)} fusion(f32[12,12]{1,0:T(8,128)S(1)} %copy-done.6, f32[8,65536]{1,0:T(8,128)S(1)} %bitcast.194, f32[12,65536]{1,0:T(8,128)S(1)} %fusion.4, f32[12]{0:T(128)S(1)} %get-tuple-element.28), kind=kOutput, calls=%fused_computation.6 | convolution fusion | flops 117178368 | bytes 8389232 | tf_op jit(solution)/shard_map/dot_general | solution.py:37
  542.5 5.0 fusion.1
  (99 shorter events, 91.3 us)
Async XLA Ops:
  0.0 47.7 %copy-start = (f32[32,32]{1,0:T(8,128)S(1)}, f32[32,32]{1,0:T(8,128)}, u32[]{:S(2)}) copy-start(f32[32,32]{1,0:T(8,128)} %param.11) | copy-start | bytes 12292
  0.7 8.6 %copy-start.10 = (f32[33]{0:T(128)S(1)}, f32[33]{0:T(128)}, u32[]{:S(2)}) copy-start(f32[33]{0:T(128)} %param.13) | copy-start | bytes 400
  0.7 19.9 %collective-permute-start = (f32[32,8]{1,0:T(8,128)S(1)}, f32[32,8]{1,0:T(8,128)S(1)}, u32[]{:S(2)}, u32[]{:S(2)}) collective-permute-start(f32[32,8]{1,0:T(8,128)S(1)} %slice.133), channel_id=1, source_target_pairs={{0,127},{1,0},{2,1},{3,2},{4,3},{5,4},{6,5},{7,6},{8,7},{9,8},{10,... | collective-permute-start | bytes 3080 | tf_op jit(solution)/shard_map/ppermute | solution.py:19
  10.0 9.4 %copy-start.7 = (f32[2]{0:T(128)S(1)}, f32[2]{0:T(128)}, u32[]{:S(2)}) copy-start(f32[2]{0:T(128)} %param.14) | copy-start | bytes 28
  14.6 4.0 copy-start.2
  30.7 17.0 %copy-start.9 = (f32[32]{0:T(128)S(1)}, f32[32]{0:T(128)}, u32[]{:S(2)}) copy-start(f32[32]{0:T(128)} %param.12) | copy-start | bytes 388
  35.5 28.8 %all-to-all-start = ((f32[128,1,1]{2,1,0:T(1,128)}), f32[128,1,1]{2,1,0:T(1,128)S(1)}, u32[]{:S(2)}, u32[]{:S(2)}) async-start(f32[128,1,1]{2,1,0:T(1,128)} %broadcast_in_dim.4), calls=%async_computation | async-start | bytes 131072 | tf_op jit(solution)/shard_map/all_to_all | solution.py:25
  68.6 20.7 %all-to-all-start.1 = ((f32[1,128,512]{2,0,1:T(1,128)}), f32[1,128,512]{2,0,1:T(1,128)S(1)}, u32[]{:S(2)}, u32[]{:S(2)}) async-start(f32[1,128,512]{2,0,1:T(1,128)} %bitcast.19), calls=%async_computation.1 | async-start | bytes 524288 | tf_op jit(solution)/shard_map/all_to_all | solution.py:83
  138.7 14.0 %all-to-all-start.3 = ((f32[2,8,1,8192]{3,0,2,1:T(2,128)}), f32[2,8,1,8192]{3,0,2,1:T(2,128)S(1)}, u32[]{:S(2)}, u32[]{:S(2)}) async-start(f32[2,8,1,8192]{3,0,2,1:T(2,128)} %copy.63), calls=%async_computation.3 | async-start | bytes 1048576 | tf_op jit(solution)/shard_map/all_to_all | solution.py:87
  205.1 23.1 %copy-start.3 = (f32[8,512,128]{2,1,0:T(8,128)}, f32[8,512,128]{2,1,0:T(8,128)S(1)}, u32[]{:S(2)}) copy-start(f32[8,512,128]{2,1,0:T(8,128)S(1)} %convolution_subtract_fusion.1) | copy-start | bytes 6291460
  274.7 45.5 %copy-start.4 = (f32[1,8,512,128]{3,2,0,1:T(8,128)S(1)}, f32[1,8,512,128]{3,2,0,1:T(8,128)}, u32[]{:S(2)}) copy-start(f32[1,8,512,128]{3,2,0,1:T(8,128)} %copy.76) | copy-start | bytes 6291460
  336.5 45.6 %copy-start.5 = (f32[1,16,1,32768]{3,1,2,0:T(8,128)S(1)}, f32[1,16,1,32768]{3,1,2,0:T(8,128)}, u32[]{:S(2)}) copy-start(f32[1,16,1,32768]{3,1,2,0:T(8,128)} %reshape.486) | copy-start | bytes 6291460
  470.8 7.0 %copy-start.8 = (f32[2,12]{1,0:T(2,128)S(1)}, f32[2,12]{1,0:T(2,128)}, u32[]{:S(2)}) copy-start(f32[2,12]{1,0:T(2,128)} %param.17) | copy-start | bytes 292
  470.8 55.8 %all-to-all-start.5 = ((f32[2,8,1,16,4096]{4,3,2,0,1:T(8,128)}), f32[2,8,1,16,4096]{4,3,2,0,1:T(8,128)}, u32[]{:S(2)}, u32[]{:S(2)}) async-start(f32[2,8,1,16,4096]{4,3,2,0,1:T(8,128)} %maximum_bitcast_fusion), calls=%async_computation.5 | async-start | bytes 8388608 | tf_op jit(solution)/shard_map/all_to_all | solution.py:87
  530.4 1.2 copy-start.6
  547.5 6.7 %copy-start.1 = (f32[32,32]{1,0:T(8,128)S(1)}, f32[32,32]{1,0:T(8,128)}, u32[]{:S(2)}) copy-start(f32[32,32]{1,0:T(8,128)} %param.11) | copy-start | bytes 12292

commit v2 on v1

--- a/solution.py
+++ b/solution.py
@@ -77,6 +77,37 @@
     final_re = jnp.swapaxes(final_re, -1, -2).reshape(leading + (length,))
     final_im = jnp.swapaxes(final_im, -1, -2).reshape(leading + (length,))
     return (final_re, final_im)
+
+
+def lift_dft(values_re, values_im, sign):
+    segs, phases, length = values_re.shape
+    first = 128
+    second = length // first
+    block_re = values_re.reshape(segs, phases, first, second)
+    block_im = values_im.reshape(segs, phases, first, second)
+    index_one = jnp.arange(first, dtype=jnp.int32)
+    index_two = jnp.arange(second, dtype=jnp.int32)
+    cos_one, sin_one = turns(index_one[:, None] * index_one[None, :], first, sign)
+    section_re = jnp.einsum("kn,spnm->skpm", cos_one, block_re, precision=highest) - jnp.einsum(
+        "kn,spnm->skpm", sin_one, block_im, precision=highest
+    )
+    section_im = jnp.einsum("kn,spnm->skpm", cos_one, block_im, precision=highest) + jnp.einsum(
+        "kn,spnm->skpm", sin_one, block_re, precision=highest
+    )
+    twist_cos, twist_sin = turns(index_one[:, None] * index_two[None, :], length, sign)
+    section_re, section_im = complex_mul(
+        section_re, section_im, twist_cos[:, None, :], twist_sin[:, None, :]
+    )
+    section_re = section_re.reshape(segs, first * phases, second)
+    section_im = section_im.reshape(segs, first * phases, second)
+    cos_two, sin_two = turns(index_two[:, None] * index_two[None, :], second, sign)
+    final_re = jnp.einsum("jm,sxm->sjx", cos_two, section_re, precision=highest) - jnp.einsum(
+        "jm,sxm->sjx", sin_two, section_im, precision=highest
+    )
+    final_im = jnp.einsum("jm,sxm->sjx", sin_two, section_re, precision=highest) + jnp.einsum(
+        "jm,sxm->sjx", cos_two, section_im, precision=highest
+    )
+    return (final_re.reshape(segs, length * phases), final_im.reshape(segs, length * phases))
 
 
 def regroup(values):
@@ -152,9 +183,7 @@
     spread_re, spread_im = complex_mul(
         owned[0][:, None, :], owned[1][:, None, :], phase_cos, phase_sin
     )
-    lift_re, lift_im = local_dft(spread_re, spread_im, 1.0)
-    lift_re = jnp.swapaxes(lift_re, 1, 2).reshape(seg_dev, band)
-    lift_im = jnp.swapaxes(lift_im, 1, 2).reshape(seg_dev, band)
+    lift_re, lift_im = lift_dft(spread_re, spread_im, 1.0)
     band_index = jnp.arange(band, dtype=jnp.int32)
     shift_cos, shift_sin = turns(band_index * row_index, total_rows, 1.0)
     lift_re, lift_im = complex_mul(lift_re, lift_im, shift_cos, shift_sin)

time: 561 us -> 433 us (0.77)
  local copies, waits for them, and re-layouts: 185 us -> 62.6 us
  matrix products: 164 us -> 158 us
    reshape x3, local copies, waits for them, and re-layouts: 91.2 us -> 3.21 us  [the longest x1 1.55 us: lift_dft(): final_re.reshape(segs, length * phases)]
    dot_general x0 -> x8, matrix products: none -> 81.3 us  [the longest x1 12.2 us: lift_dft(): jnp.einsum('jm,sxm->sjx', cos_two, section_re, precision=highest)]
    transpose x4 -> x0, local copies, waits for them, and re-layouts: 37.4 us -> none  [the longest x1 16.3 us: on_device(): lift_re = jnp.swapaxes(lift_re, 1, 2).reshape(seg_dev, band)]
    dot_general x2 -> x1, matrix products: 19.9 us -> 5.99 us  [local_dft(): jnp.einsum('...kn,jn->...kj', section_im, sin_two, precision=highest)]
    dot_general x2 -> x1, matrix products: 18.2 us -> 6.18 us  [local_dft(): jnp.einsum('...kn,jn->...kj', section_re, cos_two, precision=highest)]
    dot_general x2 -> x1, matrix products: 17.6 us -> 5.8 us  [local_dft(): jnp.einsum('...kn,jn->...kj', section_im, cos_two, precision=highest)]
    dot_general x2 -> x1, matrix products: 16.7 us -> 5.81 us  [local_dft(): jnp.einsum('...kn,jn->...kj', section_re, sin_two, precision=highest)]
    dot_general x2 -> x1, matrix products: 10.4 us -> 0.65 us  [local_dft(): jnp.einsum('kn,...nm->...km', sin_one, block_re, precision=highest)]
  transfers between devices with their start and end apart: 5 -> 5, of which waited for: 3 -> 3; matrix products, arithmetic and copies ran while one was open for 6% -> 7% of each run, Pallas kernels for 0% -> 0%
where the time goes in v2:
time: 433 us; the launch traced here: 427 us
  matrix products  158 us (36%)
  blocking collectives  71 us (16%)
  waiting for transfers between devices  67.9 us (16%)
  local copies, waits for them, and re-layouts  62.6 us (14%)
  starting transfers between devices  34.8 us (8%)
  other arithmetic  30.7 us (7%)
    all_to_all x2, waiting for transfers between devices, column_relay(): lax.all_to_all(values, 'cols', split_axis=1, concat_axis=1, tiled=True)  57.1 us
    all_to_all x1, blocking collectives, on_device(): lax.all_to_all(pieces, 'rows', split_axis=1, concat_axis=1, tiled=True)  52.9 us
    dot_general x4, matrix products, permute(): jnp.dot(hash_mds, squash(state), precision=highest, preferred_element_typ...  20.8 us
    unnamed x25, local copies, waits for them, and re-layouts  19.6 us
    all_to_all x1, blocking collectives, regroup(): lax.all_to_all(values, ('rows', 'cols'), split_axis=1, concat_axis=1, til...  18.1 us
    dot_general x1, matrix products, on_device(): jnp.dot(mds, trace, precision=highest, preferred_element_type=jnp.float32)  15.9 us
    dot_general x1, matrix products, lift_dft(): jnp.einsum('jm,sxm->sjx', cos_two, section_re, precision=highest)  12.2 us
    all_to_all x1, starting transfers between devices, entering(): pieces = lax.all_to_all(spread, axis, 0, 0, tiled=True)  11.9 us
  transfers between devices with their start and end apart: 5, of which 3 were waited for; matrix products, arithmetic and copies ran while one was open for 7% of the time, Pallas kernels for 0%

profile of v2, /device:TPU:1, one launch (start us, length us, event | category | flops | bytes accessed | tf_op | source)
XLA Modules:
  0.0 426.8 jit_solution(15568250091949918416)
XLA Ops:
  2.1 7.3 %constant_dynamic-update-slice_fusion.1 = f32[32,65544]{1,0:T(8,128)} fusion(f32[32,65536]{1,0:T(8,128)} %param.9), kind=kLoop, calls=%fused_computation.223 | loop fusion | bytes 16777216
  9.4 4.7 %convert_element_type.119 = f32[33,65536]{1,0:T(8,128)S(1)} convert(s32[33,65536]{1,0:T(8,128)} %param.10) | non-fusion elementwise | flops 2162688 | bytes 17301504 | tf_op jit(solution)/shard_map/convert_element_type | solution.py:148
  20.8 5.5 %log_subtract_fusion = (f32[1,65544]{1,0:T(1,128)S(1)}, f32[1,65544]{1,0:T(1,128)S(1)}, f32[1,65544]{1,0:T(1,128)S(1)}) fusion(f32[32,65544]{1,0:T(8,128)} %constant_dynamic-update-slice_fusion, f32[]{:T(128)} %bitcast.3, f32[]{:T(128)} %bitcast.2), kind=kLoop, calls=%fused_computation.143 | loop fusion | flops 589896 | bytes 1835240 | tf_op jit(solution)/shard_map/sub | solution.py:139
  35.0 11.9 %all-to-all-start = ((f32[128,1,1]{2,1,0:T(1,128)}), f32[128,1,1]{2,1,0:T(1,128)S(1)}, u32[]{:S(2)}, u32[]{:S(2)}) async-start(f32[128,1,1]{2,1,0:T(1,128)} %broadcast_in_dim.4), calls=%async_computation | async-start | bytes 131072 | tf_op jit(solution)/shard_map/all_to_all | solution.py:25
  46.9 15.9 %fusion.7 = f32[65536]{0:T(1024)S(1)} fusion(f32[32,65536]{1,0:T(8,128)} %param.9, f32[32,65544]{1,0:T(8,128)} %constant_dynamic-update-slice_fusion, f32[33,65536]{1,0:T(8,128)} %copy-done.2, f32[32]{0:T(128)S(1)} %copy-done.6, f32[32]{0:T(128)S(1)} %bitcast.181, f32[32,32]{1,0:T(8,128)S(1)} %copy-done), kind=kOutput, calls=%fused_computation.14 | convolution fusion | flops 819920896 | bytes 33820928 | tf_op jit(solution)/shard_map/dot_general | solution.py:133
  67.8 9.9 %all-to-all-start.1 = ((f32[1,128,512]{2,0,1:T(1,128)}), f32[1,128,512]{2,0,1:T(1,128)S(1)}, u32[]{:S(2)}, u32[]{:S(2)}) async-start(f32[1,128,512]{2,0,1:T(1,128)} %bitcast.19), calls=%async_computation.1 | async-start | bytes 524288 | tf_op jit(solution)/shard_map/all_to_all | solution.py:114
  77.7 10.8 %all-to-all-done.1 = f32[1,128,512]{2,0,1:T(1,128)S(1)} async-done(((f32[1,128,512]{2,0,1:T(1,128)}), f32[1,128,512]{2,0,1:T(1,128)S(1)}, u32[]{:S(2)}, u32[]{:S(2)}) %all-to-all-start.1) | async-done | bytes 262176 | tf_op jit(solution)/shard_map/all_to_all | solution.py:114
  91.6 18.1 %all_to_all.42 = f32[2,128,512]{2,0,1:T(2,128)S(1)} all-to-all(f32[2,128,512]{2,0,1:T(2,128)S(1)} %copy.40), channel_id=1, replica_groups=mesh['rows'=16,'cols'=8] {'rows','cols'}, dimensions={1} | all-to-all | bytes 1048576 | tf_op jit(solution)/shard_map/all_to_all | solution.py:114
  112.7 5.8 %fusion.81 = f32[512,128]{1,0:T(8,128)S(1)} fusion(f32[128,512]{1,0:T(8,128)S(1)} %convolution_add_fusion.6, f32[128,512]{1,0:T(8,128)S(1)} %convolution_subtract_fusion.2), kind=kOutput, calls=%fused_computation.122 | convolution fusion | flops 407437312 | bytes 786432 | tf_op jit(solution)/shard_map/...kn,jn->...kj/dot_general | solution.py:74
  118.5 6.2 %fusion.80 = f32[512,128]{1,0:T(8,128)S(1)} fusion(f32[128,512]{1,0:T(8,128)S(1)} %convolution_add_fusion.6, f32[128,512]{1,0:T(8,128)S(1)} %convolution_subtract_fusion.2), kind=kOutput, calls=%fused_computation.121 | convolution fusion | flops 407437312 | bytes 786432 | tf_op jit(solution)/shard_map/...kn,jn->...kj/dot_general | solution.py:71
  124.7 5.8 %fusion.63 = f32[512,128]{1,0:T(8,128)S(1)} fusion(f32[512,128]{1,0:T(8,128)S(1)} %fusion.81, f32[128,512]{1,0:T(8,128)S(1)} %convolution_add_fusion.6, f32[128,512]{1,0:T(8,128)S(1)} %convolution_subtract_fusion.2), kind=kOutput, calls=%fused_computation.98 | convolution fusion | flops 407568384 | bytes 1048576 | tf_op jit(solution)/shard_map/...kn,jn->...kj/dot_general | solution.py:74
  130.5 6.0 %fusion.64 = f32[512,128]{1,0:T(8,128)S(1)} fusion(f32[512,128]{1,0:T(8,128)S(1)} %fusion.80, f32[128,512]{1,0:T(8,128)S(1)} %convolution_add_fusion.6, f32[128,512]{1,0:T(8,128)S(1)} %convolution_subtract_fusion.2), kind=kOutput, calls=%fused_computation.100 | convolution fusion | flops 407568384 | bytes 1048576 | tf_op jit(solution)/shard_map/...kn,jn->...kj/dot_general | solution.py:71
  137.8 4.7 %all-to-all-start.3 = ((f32[2,8,1,8192]{3,0,2,1:T(2,128)}), f32[2,8,1,8192]{3,0,2,1:T(2,128)S(1)}, u32[]{:S(2)}, u32[]{:S(2)}) async-start(f32[2,8,1,8192]{3,0,2,1:T(2,128)} %copy.41), calls=%async_computation.3 | async-start | bytes 1048576 | tf_op jit(solution)/shard_map/all_to_all | solution.py:118
  143.6 8.3 %all-to-all-done.3 = f32[2,8,1,8192]{3,0,2,1:T(2,128)S(1)} async-done(((f32[2,8,1,8192]{3,0,2,1:T(2,128)}), f32[2,8,1,8192]{3,0,2,1:T(2,128)S(1)}, u32[]{:S(2)}, u32[]{:S(2)}) %all-to-all-start.3) | async-done | bytes 524320 | tf_op jit(solution)/shard_map/all_to_all | solution.py:118
  161.6 4.2 mul.785
  165.7 9.6 %fusion.71 = f32[8,512,128]{1,2,0:T(8,128)S(1)} fusion(f32[128,512]{1,0:T(8,128)S(1)} %mul.796, s32[128,512]{1,0:T(8,128)S(1)} %multiply_add_fusion.6, f32[128,512]{1,0:T(8,128)S(1)} %mul.785), kind=kOutput, calls=%fused_computation.108 | convolution fusion | flops 814448640 | bytes 2883584 | tf_op jit(solution)/shard_map/kn,spnm->skpm/dot_general | solution.py:91
  175.4 10.0 %fusion.72 = f32[8,512,128]{1,2,0:T(8,128)S(1)} fusion(f32[128,512]{1,0:T(8,128)S(1)} %mul.796, s32[128,512]{1,0:T(8,128)S(1)} %multiply_add_fusion.6, f32[128,512]{1,0:T(8,128)S(1)} %mul.785), kind=kOutput, calls=%fused_computation.109 | convolution fusion | flops 814448640 | bytes 2883584 | tf_op jit(solution)/shard_map/kn,spnm->skpm/dot_general | solution.py:94
  185.4 9.9 %convolution_subtract_fusion.1 = f32[8,512,128]{1,2,0:T(8,128)S(1)} fusion(f32[8,512,128]{1,2,0:T(8,128)S(1)} %fusion.71, f32[128,512]{1,0:T(8,128)S(1)} %mul.796, s32[128,512]{1,0:T(8,128)S(1)} %multiply_add_fusion.6, f32[128,512]{1,0:T(8,128)S(1)} %mul.785), kind=kOutput, calls=%fused_computation.91 | convolution fusion | flops 814972928 | bytes 4980736 | tf_op jit(solution)/shard_map/kn,spnm->skpm/dot_general | solution.py:91
  195.4 10.7 %fusion.38 = (f32[1,128,8,512]{3,1,2,0:T(8,128)S(1)}, f32[1,128,8,512]{3,1,2,0:T(8,128)S(1)}) fusion(f32[8,512,128]{1,2,0:T(8,128)S(1)} %convolution_subtract_fusion.1, f32[128,512]{1,0:T(8,128)S(1)} %get-tuple-element.34, f32[128,512]{1,0:T(8,128)S(1)} %get-tuple-element.35, f32[8,512,128]{1,2,0:T(8,128)S(1)} %fusion.72, f32[128,512]{1,0:T(8,128)S(1)} %mul.796, ...), kind=kOutput, calls=%fused_computation.61 | convolution fusion | flops 818118656 | bytes 9699328 | tf_op jit(solution)/shard_map/kn,spnm->skpm/dot_general | solution.py:94
  206.1 8.6 %fusion.34 = f32[1024,512]{1,0:T(8,128)S(1)} fusion(f32[1,128,8,512]{3,1,2,0:T(8,128)S(1)} %get-tuple-element.9), kind=kOutput, calls=%fused_computation.55 | convolution fusion | flops 3224895488 | bytes 4194304 | tf_op jit(solution)/shard_map/jm,sxm->sjx/dot_general | solution.py:107
  214.6 10.1 %fusion.36 = f32[1024,512]{1,0:T(8,128)} fusion(f32[1,128,8,512]{3,1,2,0:T(8,128)S(1)} %get-tuple-element.9), kind=kOutput, calls=%fused_computation.57 | convolution fusion | flops 3224895488 | bytes 4194304 | tf_op jit(solution)/shard_map/jm,sxm->sjx/dot_general | solution.py:104
  224.8 10.1 %add_bitcast_fusion = f32[1,512,1024]{1,2,0:T(8,128)} fusion(f32[1024,512]{1,0:T(8,128)S(1)} %fusion.34, f32[1,128,8,512]{3,1,2,0:T(8,128)S(1)} %get-tuple-element.8), kind=kOutput, calls=%fused_computation.75 | convolution fusion | flops 3225419776 | bytes 6291456 | tf_op jit(solution)/shard_map/jm,sxm->sjx/dot_general | solution.py:107
  238.3 12.2 %subtract_bitcast_fusion = f32[1,512,1024]{1,2,0:T(8,128)} fusion(f32[1024,512]{1,0:T(8,128)} %fusion.36, f32[1,128,8,512]{3,1,2,0:T(8,128)} %copy-done.8), kind=kOutput, calls=%fused_computation.76 | convolution fusion | flops 3225419776 | bytes 6291456 | tf_op jit(solution)/shard_map/jm,sxm->sjx/dot_general | solution.py:104
  254.0 10.3 %multiply_subtract_fusion = (f32[1,16,1,32768]{3,1,2,0:T(8,128)S(1)}, f32[1,16,1,32768]{3,1,2,0:T(8,128)S(1)}) fusion(f32[1,16,1,32768]{3,1,2,0:T(8,128)} %reshape.486, f32[1,16,1,32768]{3,1,2,0:T(8,128)} %reshape.485, s32[]{:T(128)S(6)} %axis_index.17), kind=kLoop, calls=%fused_computation.74 | loop fusion | flops 11534336 | bytes 8388612 | tf_op jit(solution)/shard_map/sub | solution.py:49
  264.6 6.3 %copy.48 = f32[2,16,1,32768]{3,2,0,1:T(1,128)} copy(f32[2,16,1,32768]{3,1,2,0:T(8,128)S(1)} %pad_maximum_fusion) | data formatting | bytes 8388608 | tf_op jit(solution)/shard_map/stack | solution.py:190
  270.9 52.9 %all_to_all.43 = f32[2,16,1,32768]{3,2,0,1:T(1,128)S(1)} all-to-all(f32[2,16,1,32768]{3,2,0,1:T(1,128)} %copy.48), channel_id=1, replica_groups=mesh['rows'=16,'cols'=8] {'rows'}, dimensions={1} | all-to-all | bytes 8388608 | tf_op jit(solution)/shard_map/all_to_all | solution.py:196
  343.2 7.0 %all-to-all-start.5 = ((f32[2,8,1,16,4096]{4,3,2,0,1:T(8,128)}), f32[2,8,1,16,4096]{4,3,2,0,1:T(8,128)}, u32[]{:S(2)}, u32[]{:S(2)}) async-start(f32[2,8,1,16,4096]{4,3,2,0,1:T(8,128)} %maximum_bitcast_fusion), calls=%async_computation.5 | async-start | bytes 8388608 | tf_op jit(solution)/shard_map/all_to_all | solution.py:118
  350.2 48.8 %all-to-all-done.5 = f32[2,8,1,16,4096]{4,3,2,0,1:T(8,128)} async-done(((f32[2,8,1,16,4096]{4,3,2,0,1:T(8,128)}), f32[2,8,1,16,4096]{4,3,2,0,1:T(8,128)}, u32[]{:S(2)}, u32[]{:S(2)}) %all-to-all-start.5) | async-done | bytes 4194336 | tf_op jit(solution)/shard_map/all_to_all | solution.py:118
  404.0 5.3 %fusion.4 = f32[12,65536]{1,0:T(8,128)S(1)} fusion(f32[12,12]{1,0:T(8,128)S(1)} %copy-done.3, f32[8,65536]{1,0:T(8,128)S(1)} %bitcast.165, f32[12]{0:T(128)S(1)} %get-tuple-element.31), kind=kOutput, calls=%fused_computation.8 | convolution fusion | flops 116391936 | bytes 5243504 | tf_op jit(solution)/shard_map/dot_general | solution.py:37
  409.3 5.6 %fusion.3 = f32[12,65536]{1,0:T(8,128)S(1)} fusion(f32[12,12]{1,0:T(8,128)S(1)} %copy-done.3, f32[8,65536]{1,0:T(8,128)S(1)} %bitcast.161, f32[12,65536]{1,0:T(8,128)S(1)} %fusion.4, f32[12]{0:T(128)S(1)} %get-tuple-element.30), kind=kOutput, calls=%fused_computation.6 | convolution fusion | flops 117178368 | bytes 8389232 | tf_op jit(solution)/shard_map/dot_general | solution.py:37
  414.9 5.0 %fusion.1 = f32[12,65536]{1,0:T(8,128)S(1)} fusion(f32[12,12]{1,0:T(8,128)S(1)} %copy-done.3, f32[12,65536]{1,0:T(8,128)S(1)} %fusion.3, f32[12]{0:T(128)S(1)} %get-tuple-element.31), kind=kOutput, calls=%fused_computation.3 | convolution fusion | flops 116391936 | bytes 6292080 | tf_op jit(solution)/shard_map/dot_general | solution.py:37
  419.9 5.0 %fusion = f32[12,65536]{1,0:T(8,128)S(1)} fusion(f32[12,12]{1,0:T(8,128)S(1)} %copy-done.3, f32[12,65536]{1,0:T(8,128)S(1)} %fusion.1, f32[12]{0:T(128)S(1)} %get-tuple-element.30), kind=kOutput, calls=%fused_computation.1 | convolution fusion | flops 116391936 | bytes 6292080 | tf_op jit(solution)/shard_map/dot_general | solution.py:37
  (88 shorter events, 73.0 us)
Async XLA Ops:
  0.0 46.8 %copy-start = (f32[32,32]{1,0:T(8,128)S(1)}, f32[32,32]{1,0:T(8,128)}, u32[]{:S(2)}) copy-start(f32[32,32]{1,0:T(8,128)} %param.11) | copy-start | bytes 12292
  0.7 19.4 %collective-permute-start = (f32[32,8]{1,0:T(8,128)S(1)}, f32[32,8]{1,0:T(8,128)S(1)}, u32[]{:S(2)}, u32[]{:S(2)}) collective-permute-start(f32[32,8]{1,0:T(8,128)S(1)} %slice.133), channel_id=1, source_target_pairs={{0,127},{1,0},{2,1},{3,2},{4,3},{5,4},{6,5},{7,6},{8,7},{9,8},{10,... | collective-permute-start | bytes 3080 | tf_op jit(solution)/shard_map/ppermute | solution.py:19
  9.4 4.7 %copy-start.7 = (f32[33]{0:T(128)S(1)}, f32[33]{0:T(128)}, u32[]{:S(2)}) copy-start(f32[33]{0:T(128)} %param.13) | copy-start | bytes 400
  9.4 9.5 %copy-start.4 = (f32[2]{0:T(128)S(1)}, f32[2]{0:T(128)}, u32[]{:S(2)}) copy-start(f32[2]{0:T(128)} %param.14) | copy-start | bytes 28
  14.1 4.0 copy-start.2
  30.1 16.7 %copy-start.6 = (f32[32]{0:T(128)S(1)}, f32[32]{0:T(128)}, u32[]{:S(2)}) copy-start(f32[32]{0:T(128)} %param.12) | copy-start | bytes 388
  35.0 28.5 %all-to-all-start = ((f32[128,1,1]{2,1,0:T(1,128)}), f32[128,1,1]{2,1,0:T(1,128)S(1)}, u32[]{:S(2)}, u32[]{:S(2)}) async-start(f32[128,1,1]{2,1,0:T(1,128)} %broadcast_in_dim.4), calls=%async_computation | async-start | bytes 131072 | tf_op jit(solution)/shard_map/all_to_all | solution.py:25
  67.8 20.7 %all-to-all-start.1 = ((f32[1,128,512]{2,0,1:T(1,128)}), f32[1,128,512]{2,0,1:T(1,128)S(1)}, u32[]{:S(2)}, u32[]{:S(2)}) async-start(f32[1,128,512]{2,0,1:T(1,128)} %bitcast.19), calls=%async_computation.1 | async-start | bytes 524288 | tf_op jit(solution)/shard_map/all_to_all | solution.py:114
  137.8 14.0 %all-to-all-start.3 = ((f32[2,8,1,8192]{3,0,2,1:T(2,128)}), f32[2,8,1,8192]{3,0,2,1:T(2,128)S(1)}, u32[]{:S(2)}, u32[]{:S(2)}) async-start(f32[2,8,1,8192]{3,0,2,1:T(2,128)} %copy.41), calls=%async_computation.3 | async-start | bytes 1048576 | tf_op jit(solution)/shard_map/all_to_all | solution.py:118
  206.0 18.7 %copy-start.8 = (f32[1,128,8,512]{3,1,2,0:T(8,128)}, f32[1,128,8,512]{3,1,2,0:T(8,128)S(1)}, u32[]{:S(2)}) copy-start(f32[1,128,8,512]{3,1,2,0:T(8,128)S(1)} %get-tuple-element.8) | copy-start | bytes 6291460
  343.2 7.0 %copy-start.5 = (f32[2,12]{1,0:T(2,128)S(1)}, f32[2,12]{1,0:T(2,128)}, u32[]{:S(2)}) copy-start(f32[2,12]{1,0:T(2,128)} %param.17) | copy-start | bytes 292
  343.2 55.8 %all-to-all-start.5 = ((f32[2,8,1,16,4096]{4,3,2,0,1:T(8,128)}), f32[2,8,1,16,4096]{4,3,2,0,1:T(8,128)}, u32[]{:S(2)}, u32[]{:S(2)}) async-start(f32[2,8,1,16,4096]{4,3,2,0,1:T(8,128)} %maximum_bitcast_fusion), calls=%async_computation.5 | async-start | bytes 8388608 | tf_op jit(solution)/shard_map/all_to_all | solution.py:118
  402.8 1.2 copy-start.3
  419.9 6.7 %copy-start.1 = (f32[32,32]{1,0:T(8,128)S(1)}, f32[32,32]{1,0:T(8,128)}, u32[]{:S(2)}) copy-start(f32[32,32]{1,0:T(8,128)} %param.11) | copy-start | bytes 12292

commit v3 on v2

--- a/solution.py
+++ b/solution.py
@@ -187,26 +187,22 @@
     band_index = jnp.arange(band, dtype=jnp.int32)
     shift_cos, shift_sin = turns(band_index * row_index, total_rows, 1.0)
     lift_re, lift_im = complex_mul(lift_re, lift_im, shift_cos, shift_sin)
-    lifted = jnp.stack([lift_re, lift_im])
-    slab = band // n_rows
     small = band // devices
+    lifted = (
+        jnp.stack([lift_re, lift_im])
+        .reshape(2, seg_dev, devices, small)
+        .transpose(0, 2, 1, 3)
+    )
+    arrived = regroup(lifted).reshape(2, n_rows, n_cols, seg_dev, small)
     row_ids = jnp.arange(n_rows, dtype=jnp.int32)
     cos_rows, sin_rows = turns(row_ids[:, None] * row_ids[None, :], n_rows, 1.0)
-    pieces = lifted.reshape(2, seg_dev, n_rows, slab).transpose(0, 2, 1, 3)
-    arrived = lax.all_to_all(pieces, "rows", split_axis=1, concat_axis=1, tiled=True)
-    summed_re = jnp.einsum("ab,b...->a...", cos_rows, arrived[0], precision=highest) - jnp.einsum(
-        "ab,b...->a...", sin_rows, arrived[1], precision=highest
-    )
-    summed_im = jnp.einsum("ab,b...->a...", sin_rows, arrived[0], precision=highest) + jnp.einsum(
-        "ab,b...->a...", cos_rows, arrived[1], precision=highest
-    )
-    outgoing = (
-        jnp.stack([summed_re, summed_im])
-        .reshape(2, n_rows, seg_dev, n_cols, small)
-        .transpose(0, 3, 2, 1, 4)
-    )
-    landed = column_relay(outgoing)
-    values = landed.reshape(2, SEGMENTS, n_rows, small)
+    summed_re = jnp.einsum("ab,bcsu->csau", cos_rows, arrived[0], precision=highest) - jnp.einsum(
+        "ab,bcsu->csau", sin_rows, arrived[1], precision=highest
+    )
+    summed_im = jnp.einsum("ab,bcsu->csau", sin_rows, arrived[0], precision=highest) + jnp.einsum(
+        "ab,bcsu->csau", cos_rows, arrived[1], precision=highest
+    )
+    values = jnp.stack([summed_re, summed_im]).reshape(2, SEGMENTS, n_rows, small)
     leaf_count = n_rows * small
     real_part = values[0].reshape(SEGMENTS, leaf_count)
     imag_part = values[1].reshape(SEGMENTS, leaf_count)

time: 433 us -> 384 us (0.89)
  blocking collectives: 71 us -> 18.1 us
    all_to_all x1 -> x0, blocking collectives: 52.9 us -> none  [on_device(): lax.all_to_all(pieces, 'rows', split_axis=1, concat_axis=1, tiled=True)]
    all_to_all x1 -> x2, waiting for transfers between devices: 10.8 us -> 63.2 us  [regroup(): lax.all_to_all(values, ('rows', 'cols'), split_axis=1, concat_axis=1, til...]
    all_to_all x2 -> x1, waiting for transfers between devices: 57.1 us -> 8.31 us  [column_relay(): lax.all_to_all(values, 'cols', split_axis=1, concat_axis=1, tiled=True)]
    all_to_all x2 -> x1, starting transfers between devices: 11.7 us -> 4.65 us  [column_relay(): lax.all_to_all(values, 'cols', split_axis=1, concat_axis=1, tiled=True)]
    all_to_all x1 -> x2, starting transfers between devices: 9.9 us -> 16 us  [regroup(): lax.all_to_all(values, ('rows', 'cols'), split_axis=1, concat_axis=1, til...]
    slice x1, local copies, waits for them, and re-layouts: 0.44 us -> 6.01 us  [on_device(): arrived[1]]
    another operation x7 -> x5, local copies, waits for them, and re-layouts: 10 us -> 7.68 us  [the longest x1 6.35 us: on_device(): jnp.stack([lift_re, lift_im]).reshape(2, seg_dev, devices, small)]
    unnamed x25 -> x24, local copies, waits for them, and re-layouts: 19.6 us -> 17.9 us
  transfers between devices with their start and end apart: 5 -> 5, of which waited for: 3 -> 3; matrix products, arithmetic and copies ran while one was open for 7% -> 8% of each run, Pallas kernels for 0% -> 0%
where the time goes in v3:
time: 384 us; the launch traced here: 378 us
  matrix products  159 us (41%)
  waiting for transfers between devices  71.5 us (19%)
  local copies, waits for them, and re-layouts  65.2 us (17%)
  starting transfers between devices  33.9 us (9%)
  other arithmetic  28.5 us (7%)
  blocking collectives  18.1 us (5%)
    all_to_all x2, waiting for transfers between devices, regroup(): lax.all_to_all(values, ('rows', 'cols'), split_axis=1, concat_axis=1, til...  63.2 us
    dot_general x4, matrix products, permute(): jnp.dot(hash_mds, squash(state), precision=highest, preferred_element_typ...  21.1 us
    all_to_all x1, blocking collectives, regroup(): lax.all_to_all(values, ('rows', 'cols'), split_axis=1, concat_axis=1, til...  18.1 us
    unnamed x24, local copies, waits for them, and re-layouts  17.9 us
    all_to_all x2, starting transfers between devices, regroup(): lax.all_to_all(values, ('rows', 'cols'), split_axis=1, concat_axis=1, til...  16 us
    dot_general x1, matrix products, on_device(): jnp.dot(mds, trace, precision=highest, preferred_element_type=jnp.float32)  15.9 us
    dot_general x1, matrix products, lift_dft(): jnp.einsum('jm,sxm->sjx', cos_two, section_re, precision=highest)  12.2 us
    all_to_all x1, starting transfers between devices, entering(): pieces = lax.all_to_all(spread, axis, 0, 0, tiled=True)  11.9 us
  transfers between devices with their start and end apart: 5, of which 3 were waited for; matrix products, arithmetic and copies ran while one was open for 8% of the time, Pallas kernels for 0%

profile of v3, /device:TPU:1, one launch (start us, length us, event | category | flops | bytes accessed | tf_op | source)
XLA Modules:
  0.0 378.0 jit_solution(11602780505021512360)
XLA Ops:
  2.1 7.2 %constant_dynamic-update-slice_fusion.1 = f32[32,65544]{1,0:T(8,128)} fusion(f32[32,65536]{1,0:T(8,128)} %param.9), kind=kLoop, calls=%fused_computation.224 | loop fusion | bytes 16777216
  9.4 4.7 %convert_element_type.118 = f32[33,65536]{1,0:T(8,128)S(1)} convert(s32[33,65536]{1,0:T(8,128)} %param.10) | non-fusion elementwise | flops 2162688 | bytes 17301504 | tf_op jit(solution)/shard_map/convert_element_type | solution.py:148
  20.8 5.7 %log_subtract_fusion = (f32[1,65544]{1,0:T(1,128)S(1)}, f32[1,65544]{1,0:T(1,128)S(1)}, f32[1,65544]{1,0:T(1,128)S(1)}) fusion(f32[32,65544]{1,0:T(8,128)} %constant_dynamic-update-slice_fusion, f32[]{:T(128)} %bitcast.3, f32[]{:T(128)} %bitcast.2), kind=kLoop, calls=%fused_computation.140 | loop fusion | flops 589896 | bytes 1835240 | tf_op jit(solution)/shard_map/sub | solution.py:139
  35.1 11.9 %all-to-all-start = ((f32[128,1,1]{2,1,0:T(1,128)}), f32[128,1,1]{2,1,0:T(1,128)S(1)}, u32[]{:S(2)}, u32[]{:S(2)}) async-start(f32[128,1,1]{2,1,0:T(1,128)} %broadcast_in_dim.4), calls=%async_computation | async-start | bytes 131072 | tf_op jit(solution)/shard_map/all_to_all | solution.py:25
  47.0 15.9 %fusion.7 = f32[65536]{0:T(1024)S(1)} fusion(f32[32,65536]{1,0:T(8,128)} %param.9, f32[32,65544]{1,0:T(8,128)} %constant_dynamic-update-slice_fusion, f32[33,65536]{1,0:T(8,128)} %copy-done.2, f32[32]{0:T(128)S(1)} %copy-done.6, f32[32]{0:T(128)S(1)} %bitcast.183, f32[32,32]{1,0:T(8,128)S(1)} %copy-done), kind=kOutput, calls=%fused_computation.12 | convolution fusion | flops 819920896 | bytes 33820928 | tf_op jit(solution)/shard_map/dot_general | solution.py:133
  68.1 9.9 %all-to-all-start.1 = ((f32[1,128,512]{2,0,1:T(1,128)}), f32[1,128,512]{2,0,1:T(1,128)S(1)}, u32[]{:S(2)}, u32[]{:S(2)}) async-start(f32[1,128,512]{2,0,1:T(1,128)} %bitcast.19), calls=%async_computation.1 | async-start | bytes 524288 | tf_op jit(solution)/shard_map/all_to_all | solution.py:114
  78.0 10.8 %all-to-all-done.1 = f32[1,128,512]{2,0,1:T(1,128)S(1)} async-done(((f32[1,128,512]{2,0,1:T(1,128)}), f32[1,128,512]{2,0,1:T(1,128)S(1)}, u32[]{:S(2)}, u32[]{:S(2)}) %all-to-all-start.1) | async-done | bytes 262176 | tf_op jit(solution)/shard_map/all_to_all | solution.py:114
  91.8 18.1 %all_to_all.37 = f32[2,128,512]{2,0,1:T(2,128)S(1)} all-to-all(f32[2,128,512]{2,0,1:T(2,128)S(1)} %copy.48), channel_id=1, replica_groups=mesh['rows'=16,'cols'=8] {'rows','cols'}, dimensions={1} | all-to-all | bytes 1048576 | tf_op jit(solution)/shard_map/all_to_all | solution.py:114
  112.9 5.8 %fusion.79 = f32[512,128]{1,0:T(8,128)S(1)} fusion(f32[128,512]{1,0:T(8,128)S(1)} %convolution_add_fusion.6, f32[128,512]{1,0:T(8,128)S(1)} %convolution_subtract_fusion.2), kind=kOutput, calls=%fused_computation.119 | convolution fusion | flops 407437312 | bytes 786432 | tf_op jit(solution)/shard_map/...kn,jn->...kj/dot_general | solution.py:74
  118.7 6.0 %fusion.78 = f32[512,128]{1,0:T(8,128)S(1)} fusion(f32[128,512]{1,0:T(8,128)S(1)} %convolution_add_fusion.6, f32[128,512]{1,0:T(8,128)S(1)} %convolution_subtract_fusion.2), kind=kOutput, calls=%fused_computation.118 | convolution fusion | flops 407437312 | bytes 786432 | tf_op jit(solution)/shard_map/...kn,jn->...kj/dot_general | solution.py:71
  124.7 5.8 %fusion.61 = f32[512,128]{1,0:T(8,128)S(1)} fusion(f32[512,128]{1,0:T(8,128)S(1)} %fusion.79, f32[128,512]{1,0:T(8,128)S(1)} %convolution_add_fusion.6, f32[128,512]{1,0:T(8,128)S(1)} %convolution_subtract_fusion.2), kind=kOutput, calls=%fused_computation.95 | convolution fusion | flops 407568384 | bytes 1048576 | tf_op jit(solution)/shard_map/...kn,jn->...kj/dot_general | solution.py:74
  130.5 6.0 %fusion.62 = f32[512,128]{1,0:T(8,128)S(1)} fusion(f32[512,128]{1,0:T(8,128)S(1)} %fusion.78, f32[128,512]{1,0:T(8,128)S(1)} %convolution_add_fusion.6, f32[128,512]{1,0:T(8,128)S(1)} %convolution_subtract_fusion.2), kind=kOutput, calls=%fused_computation.97 | convolution fusion | flops 407568384 | bytes 1048576 | tf_op jit(solution)/shard_map/...kn,jn->...kj/dot_general | solution.py:71
  137.9 4.7 %all-to-all-start.3 = ((f32[2,8,1,8192]{3,0,2,1:T(2,128)}), f32[2,8,1,8192]{3,0,2,1:T(2,128)S(1)}, u32[]{:S(2)}, u32[]{:S(2)}) async-start(f32[2,8,1,8192]{3,0,2,1:T(2,128)} %copy.49), calls=%async_computation.3 | async-start | bytes 1048576 | tf_op jit(solution)/shard_map/all_to_all | solution.py:118
  143.6 8.3 %all-to-all-done.3 = f32[2,8,1,8192]{3,0,2,1:T(2,128)S(1)} async-done(((f32[2,8,1,8192]{3,0,2,1:T(2,128)}), f32[2,8,1,8192]{3,0,2,1:T(2,128)S(1)}, u32[]{:S(2)}, u32[]{:S(2)}) %all-to-all-start.3) | async-done | bytes 524320 | tf_op jit(solution)/shard_map/all_to_all | solution.py:118
  161.6 4.4 %mul.780 = f32[128,512]{1,0:T(8,128)S(1)} reshape(f32[1,1,8192,8]{3,2,1,0:T(8,128)} %copy.50) | data formatting | bytes 524288 | tf_op jit(solution)/shard_map/mul | solution.py:49
  166.0 9.6 %fusion.69 = f32[8,512,128]{1,2,0:T(8,128)S(1)} fusion(f32[128,512]{1,0:T(8,128)S(1)} %mul.791, s32[128,512]{1,0:T(8,128)S(1)} %multiply_add_fusion.6, f32[128,512]{1,0:T(8,128)S(1)} %mul.780), kind=kOutput, calls=%fused_computation.105 | convolution fusion | flops 814448640 | bytes 2883584 | tf_op jit(solution)/shard_map/kn,spnm->skpm/dot_general | solution.py:91
  175.6 9.8 %fusion.70 = f32[8,512,128]{1,2,0:T(8,128)S(1)} fusion(f32[128,512]{1,0:T(8,128)S(1)} %mul.791, s32[128,512]{1,0:T(8,128)S(1)} %multiply_add_fusion.6, f32[128,512]{1,0:T(8,128)S(1)} %mul.780), kind=kOutput, calls=%fused_computation.106 | convolution fusion | flops 814448640 | bytes 2883584 | tf_op jit(solution)/shard_map/kn,spnm->skpm/dot_general | solution.py:94
  185.4 10.0 %convolution_subtract_fusion.1 = f32[8,512,128]{1,2,0:T(8,128)S(1)} fusion(f32[8,512,128]{1,2,0:T(8,128)S(1)} %fusion.69, f32[128,512]{1,0:T(8,128)S(1)} %mul.791, s32[128,512]{1,0:T(8,128)S(1)} %multiply_add_fusion.6, f32[128,512]{1,0:T(8,128)S(1)} %mul.780), kind=kOutput, calls=%fused_computation.88 | convolution fusion | flops 814972928 | bytes 4980736 | tf_op jit(solution)/shard_map/kn,spnm->skpm/dot_general | solution.py:91
  195.4 10.9 %fusion.34 = (f32[1,128,8,512]{3,1,2,0:T(8,128)S(1)}, f32[1,128,8,512]{3,1,2,0:T(8,128)S(1)}) fusion(f32[8,512,128]{1,2,0:T(8,128)S(1)} %convolution_subtract_fusion.1, f32[128,512]{1,0:T(8,128)S(1)} %get-tuple-element.32, f32[128,512]{1,0:T(8,128)S(1)} %get-tuple-element.33, f32[8,512,128]{1,2,0:T(8,128)S(1)} %fusion.70, f32[128,512]{1,0:T(8,128)S(1)} %mul.791, ...), kind=kOutput, calls=%fused_computation.56 | convolution fusion | flops 818118656 | bytes 9699328 | tf_op jit(solution)/shard_map/kn,spnm->skpm/dot_general | solution.py:94
  206.3 8.3 %fusion.30 = f32[1024,512]{1,0:T(8,128)S(1)} fusion(f32[1,128,8,512]{3,1,2,0:T(8,128)S(1)} %get-tuple-element.9), kind=kOutput, calls=%fused_computation.50 | convolution fusion | flops 3224895488 | bytes 4194304 | tf_op jit(solution)/shard_map/jm,sxm->sjx/dot_general | solution.py:107
  214.6 10.1 %fusion.32 = f32[1024,512]{1,0:T(8,128)} fusion(f32[1,128,8,512]{3,1,2,0:T(8,128)S(1)} %get-tuple-element.9), kind=kOutput, calls=%fused_computation.52 | convolution fusion | flops 3224895488 | bytes 4194304 | tf_op jit(solution)/shard_map/jm,sxm->sjx/dot_general | solution.py:104
  224.8 10.1 %add_bitcast_fusion = f32[1,512,1024]{1,2,0:T(8,128)} fusion(f32[1024,512]{1,0:T(8,128)S(1)} %fusion.30, f32[1,128,8,512]{3,1,2,0:T(8,128)S(1)} %get-tuple-element.8), kind=kOutput, calls=%fused_computation.70 | convolution fusion | flops 3225419776 | bytes 6291456 | tf_op jit(solution)/shard_map/jm,sxm->sjx/dot_general | solution.py:107
  238.8 12.2 %subtract_bitcast_fusion = f32[1,512,1024]{1,2,0:T(8,128)} fusion(f32[1024,512]{1,0:T(8,128)} %fusion.32, f32[1,128,8,512]{3,1,2,0:T(8,128)} %copy-done.8), kind=kOutput, calls=%fused_computation.71 | convolution fusion | flops 3225419776 | bytes 6291456 | tf_op jit(solution)/shard_map/jm,sxm->sjx/dot_general | solution.py:104
  254.9 10.2 %multiply_subtract_fusion = (f32[1,128,1,4096]{3,1,2,0:T(8,128)S(1)}, f32[1,128,1,4096]{3,1,2,0:T(8,128)S(1)}) fusion(f32[1,128,1,4096]{3,1,2,0:T(8,128)} %reshape.486, f32[1,128,1,4096]{3,1,2,0:T(8,128)} %reshape.485, s32[]{:T(128)S(6)} %axis_index.17), kind=kLoop, calls=%fused_computation.69 | loop fusion | flops 11534336 | bytes 8388612 | tf_op jit(solution)/shard_map/sub | solution.py:49
  265.4 6.3 %copy.56 = f32[2,128,1,4096]{3,2,0,1:T(1,128)} copy(f32[2,128,1,4096]{3,1,2,0:T(8,128)S(1)} %pad_maximum_fusion) | data formatting | bytes 8388608 | tf_op jit(solution)/shard_map/stack | solution.py:192
  271.8 6.1 %all-to-all-start.4 = ((f32[2,128,1,4096]{3,2,0,1:T(1,128)}), f32[2,128,1,4096]{3,2,0,1:T(1,128)}, u32[]{:S(2)}, u32[]{:S(2)}) async-start(f32[2,128,1,4096]{3,2,0,1:T(1,128)} %copy.56), calls=%async_computation.4 | async-start | bytes 8388608 | tf_op jit(solution)/shard_map/all_to_all | solution.py:114
  277.9 52.4 %all-to-all-done.4 = f32[2,128,1,4096]{3,2,0,1:T(1,128)} async-done(((f32[2,128,1,4096]{3,2,0,1:T(1,128)}), f32[2,128,1,4096]{3,2,0,1:T(1,128)}, u32[]{:S(2)}, u32[]{:S(2)}) %all-to-all-start.4) | async-done | bytes 4194336 | tf_op jit(solution)/shard_map/all_to_all | solution.py:114
  330.3 6.0 %fusion.290 = (f32[1,128,1,4096]{3,2,0,1:T(1,128)S(1)}, f32[1,128,1,4096]{3,2,0,1:T(1,128)S(1)}) fusion(f32[2,128,1,4096]{3,2,0,1:T(1,128)} %all-to-all-done.4), kind=kLoop, calls=%fused_computation.352 | loop fusion | bytes 8388608 | tf_op jit(solution)/shard_map/slice | solution.py:200
  354.7 5.5 %fusion.4 = f32[12,65536]{1,0:T(8,128)S(1)} fusion(f32[12,12]{1,0:T(8,128)S(1)} %copy-done.3, f32[8,65536]{1,0:T(8,128)S(1)} %bitcast.167, f32[12]{0:T(128)S(1)} %get-tuple-element.29), kind=kOutput, calls=%fused_computation.8 | convolution fusion | flops 116391936 | bytes 5243504 | tf_op jit(solution)/shard_map/dot_general | solution.py:37
  360.2 5.4 %fusion.3 = f32[12,65536]{1,0:T(8,128)S(1)} fusion(f32[12,12]{1,0:T(8,128)S(1)} %copy-done.3, f32[8,65536]{1,0:T(8,128)S(1)} %bitcast.163, f32[12,65536]{1,0:T(8,128)S(1)} %fusion.4, f32[12]{0:T(128)S(1)} %get-tuple-element.28), kind=kOutput, calls=%fused_computation.6 | convolution fusion | flops 117178368 | bytes 8389232 | tf_op jit(solution)/shard_map/dot_general | solution.py:37
  365.6 5.2 %fusion.1 = f32[12,65536]{1,0:T(8,128)S(1)} fusion(f32[12,12]{1,0:T(8,128)S(1)} %copy-done.3, f32[12,65536]{1,0:T(8,128)S(1)} %fusion.3, f32[12]{0:T(128)S(1)} %get-tuple-element.29), kind=kOutput, calls=%fused_computation.3 | convolution fusion | flops 116391936 | bytes 6292080 | tf_op jit(solution)/shard_map/dot_general | solution.py:37
  370.9 5.0 %fusion = f32[12,65536]{1,0:T(8,128)S(1)} fusion(f32[12,12]{1,0:T(8,128)S(1)} %copy-done.3, f32[12,65536]{1,0:T(8,128)S(1)} %fusion.1, f32[12]{0:T(128)S(1)} %get-tuple-element.28), kind=kOutput, calls=%fused_computation.1 | convolution fusion | flops 116391936 | bytes 6292080 | tf_op jit(solution)/shard_map/dot_general | solution.py:37
  (83 shorter events, 68.1 us)
Async XLA Ops:
  0.0 47.0 %copy-start = (f32[32,32]{1,0:T(8,128)S(1)}, f32[32,32]{1,0:T(8,128)}, u32[]{:S(2)}) copy-start(f32[32,32]{1,0:T(8,128)} %param.11) | copy-start | bytes 12292
  0.7 19.4 %collective-permute-start = (f32[32,8]{1,0:T(8,128)S(1)}, f32[32,8]{1,0:T(8,128)S(1)}, u32[]{:S(2)}, u32[]{:S(2)}) collective-permute-start(f32[32,8]{1,0:T(8,128)S(1)} %slice.131), channel_id=1, source_target_pairs={{0,127},{1,0},{2,1},{3,2},{4,3},{5,4},{6,5},{7,6},{8,7},{9,8},{10,... | collective-permute-start | bytes 3080 | tf_op jit(solution)/shard_map/ppermute | solution.py:19
  9.3 4.7 %copy-start.7 = (f32[33]{0:T(128)S(1)}, f32[33]{0:T(128)}, u32[]{:S(2)}) copy-start(f32[33]{0:T(128)} %param.13) | copy-start | bytes 400
  9.3 9.5 %copy-start.4 = (f32[2]{0:T(128)S(1)}, f32[2]{0:T(128)}, u32[]{:S(2)}) copy-start(f32[2]{0:T(128)} %param.14) | copy-start | bytes 28
  14.0 4.0 %copy-start.2 = (f32[33,65536]{1,0:T(8,128)}, f32[33,65536]{1,0:T(8,128)S(1)}, u32[]{:S(2)}) copy-start(f32[33,65536]{1,0:T(8,128)S(1)} %convert_element_type.118) | copy-start | bytes 25952260
  30.3 16.8 %copy-start.6 = (f32[32]{0:T(128)S(1)}, f32[32]{0:T(128)}, u32[]{:S(2)}) copy-start(f32[32]{0:T(128)} %param.12) | copy-start | bytes 388
  35.1 28.6 %all-to-all-start = ((f32[128,1,1]{2,1,0:T(1,128)}), f32[128,1,1]{2,1,0:T(1,128)S(1)}, u32[]{:S(2)}, u32[]{:S(2)}) async-start(f32[128,1,1]{2,1,0:T(1,128)} %broadcast_in_dim.4), calls=%async_computation | async-start | bytes 131072 | tf_op jit(solution)/shard_map/all_to_all | solution.py:25
  68.1 20.7 %all-to-all-start.1 = ((f32[1,128,512]{2,0,1:T(1,128)}), f32[1,128,512]{2,0,1:T(1,128)S(1)}, u32[]{:S(2)}, u32[]{:S(2)}) async-start(f32[1,128,512]{2,0,1:T(1,128)} %bitcast.19), calls=%async_computation.1 | async-start | bytes 524288 | tf_op jit(solution)/shard_map/all_to_all | solution.py:114
  137.9 14.0 %all-to-all-start.3 = ((f32[2,8,1,8192]{3,0,2,1:T(2,128)}), f32[2,8,1,8192]{3,0,2,1:T(2,128)S(1)}, u32[]{:S(2)}, u32[]{:S(2)}) async-start(f32[2,8,1,8192]{3,0,2,1:T(2,128)} %copy.49), calls=%async_computation.3 | async-start | bytes 1048576 | tf_op jit(solution)/shard_map/all_to_all | solution.py:118
  206.3 18.5 %copy-start.8 = (f32[1,128,8,512]{3,1,2,0:T(8,128)}, f32[1,128,8,512]{3,1,2,0:T(8,128)S(1)}, u32[]{:S(2)}) copy-start(f32[1,128,8,512]{3,1,2,0:T(8,128)S(1)} %get-tuple-element.8) | copy-start | bytes 6291460
  271.8 6.1 %copy-start.5 = (f32[2,12]{1,0:T(2,128)S(1)}, f32[2,12]{1,0:T(2,128)}, u32[]{:S(2)}) copy-start(f32[2,12]{1,0:T(2,128)} %param.17) | copy-start | bytes 292
  271.8 58.5 %all-to-all-start.4 = ((f32[2,128,1,4096]{3,2,0,1:T(1,128)}), f32[2,128,1,4096]{3,2,0,1:T(1,128)}, u32[]{:S(2)}, u32[]{:S(2)}) async-start(f32[2,128,1,4096]{3,2,0,1:T(1,128)} %copy.56), calls=%async_computation.4 | async-start | bytes 8388608 | tf_op jit(solution)/shard_map/all_to_all | solution.py:114
  353.5 1.2 copy-start.3
  370.8 6.7 %copy-start.1 = (f32[32,32]{1,0:T(8,128)S(1)}, f32[32,32]{1,0:T(8,128)}, u32[]{:S(2)}) copy-start(f32[32,32]{1,0:T(8,128)} %param.11) | copy-start | bytes 12292

commit v4 on v3

--- a/solution.py
+++ b/solution.py
@@ -12,6 +12,7 @@
 
 
 highest = lax.Precision.HIGHEST
+three_pass = lax.Precision.HIGH
 
 
 def from_behind(array, axis, by):
@@ -59,20 +60,20 @@
     index_one = jnp.arange(first, dtype=jnp.int32)
     index_two = jnp.arange(second, dtype=jnp.int32)
     cos_one, sin_one = turns(index_one[:, None] * index_one[None, :], first, sign)
-    section_re = jnp.einsum("kn,...nm->...km", cos_one, block_re, precision=highest) - jnp.einsum(
-        "kn,...nm->...km", sin_one, block_im, precision=highest
-    )
-    section_im = jnp.einsum("kn,...nm->...km", cos_one, block_im, precision=highest) + jnp.einsum(
-        "kn,...nm->...km", sin_one, block_re, precision=highest
+    section_re = jnp.einsum("kn,...nm->...km", cos_one, block_re, precision=three_pass) - jnp.einsum(
+        "kn,...nm->...km", sin_one, block_im, precision=three_pass
+    )
+    section_im = jnp.einsum("kn,...nm->...km", cos_one, block_im, precision=three_pass) + jnp.einsum(
+        "kn,...nm->...km", sin_one, block_re, precision=three_pass
     )
     twist_cos, twist_sin = turns(index_one[:, None] * index_two[None, :], length, sign)
     section_re, section_im = complex_mul(section_re, section_im, twist_cos, twist_sin)
     cos_two, sin_two = turns(index_two[:, None] * index_two[None, :], second, sign)
-    final_re = jnp.einsum("...kn,jn->...kj", section_re, cos_two, precision=highest) - jnp.einsum(
-        "...kn,jn->...kj", section_im, sin_two, precision=highest
-    )
-    final_im = jnp.einsum("...kn,jn->...kj", section_re, sin_two, precision=highest) + jnp.einsum(
-        "...kn,jn->...kj", section_im, cos_two, precision=highest
+    final_re = jnp.einsum("...kn,jn->...kj", section_re, cos_two, precision=three_pass) - jnp.einsum(
+        "...kn,jn->...kj", section_im, sin_two, precision=three_pass
+    )
+    final_im = jnp.einsum("...kn,jn->...kj", section_re, sin_two, precision=three_pass) + jnp.einsum(
+        "...kn,jn->...kj", section_im, cos_two, precision=three_pass
     )
     final_re = jnp.swapaxes(final_re, -1, -2).reshape(leading + (length,))
     final_im = jnp.swapaxes(final_im, -1, -2).reshape(leading + (length,))
@@ -88,11 +89,11 @@
     index_one = jnp.arange(first, dtype=jnp.int32)
     index_two = jnp.arange(second, dtype=jnp.int32)
     cos_one, sin_one = turns(index_one[:, None] * index_one[None, :], first, sign)
-    section_re = jnp.einsum("kn,spnm->skpm", cos_one, block_re, precision=highest) - jnp.einsum(
-        "kn,spnm->skpm", sin_one, block_im, precision=highest
-    )
-    section_im = jnp.einsum("kn,spnm->skpm", cos_one, block_im, precision=highest) + jnp.einsum(
-        "kn,spnm->skpm", sin_one, block_re, precision=highest
+    section_re = jnp.einsum("kn,spnm->skpm", cos_one, block_re, precision=three_pass) - jnp.einsum(
+        "kn,spnm->skpm", sin_one, block_im, precision=three_pass
+    )
+    section_im = jnp.einsum("kn,spnm->skpm", cos_one, block_im, precision=three_pass) + jnp.einsum(
+        "kn,spnm->skpm", sin_one, block_re, precision=three_pass
     )
     twist_cos, twist_sin = turns(index_one[:, None] * index_two[None, :], length, sign)
     section_re, section_im = complex_mul(
@@ -101,11 +102,11 @@
     section_re = section_re.reshape(segs, first * phases, second)
     section_im = section_im.reshape(segs, first * phases, second)
     cos_two, sin_two = turns(index_two[:, None] * index_two[None, :], second, sign)
-    final_re = jnp.einsum("jm,sxm->sjx", cos_two, section_re, precision=highest) - jnp.einsum(
-        "jm,sxm->sjx", sin_two, section_im, precision=highest
-    )
-    final_im = jnp.einsum("jm,sxm->sjx", sin_two, section_re, precision=highest) + jnp.einsum(
-        "jm,sxm->sjx", cos_two, section_im, precision=highest
+    final_re = jnp.einsum("jm,sxm->sjx", cos_two, section_re, precision=three_pass) - jnp.einsum(
+        "jm,sxm->sjx", sin_two, section_im, precision=three_pass
+    )
+    final_im = jnp.einsum("jm,sxm->sjx", sin_two, section_re, precision=three_pass) + jnp.einsum(
+        "jm,sxm->sjx", cos_two, section_im, precision=three_pass
     )
     return (final_re.reshape(segs, length * phases), final_im.reshape(segs, length * phases))
 
@@ -155,8 +156,8 @@
     gathered = regroup(quotient.reshape(1, rows_dev)).reshape(devices, parts)
     block_index = jnp.arange(devices, dtype=jnp.int32)
     cos_block, sin_block = turns(block_index[:, None] * block_index[None, :], devices, -1.0)
-    first_re = jnp.dot(cos_block, gathered, precision=highest, preferred_element_type=jnp.float32)
-    first_im = jnp.dot(sin_block, gathered, precision=highest, preferred_element_type=jnp.float32)
+    first_re = jnp.dot(cos_block, gathered, precision=three_pass, preferred_element_type=jnp.float32)
+    first_im = jnp.dot(sin_block, gathered, precision=three_pass, preferred_element_type=jnp.float32)
     global_pos = flat_index * parts + jnp.arange(parts, dtype=jnp.int32)
     twist_cos, twist_sin = turns(block_index[:, None] * global_pos[None, :], total_rows, -1.0)
     first_re, first_im = complex_mul(first_re, first_im, twist_cos, twist_sin)
@@ -196,11 +197,11 @@
     arrived = regroup(lifted).reshape(2, n_rows, n_cols, seg_dev, small)
     row_ids = jnp.arange(n_rows, dtype=jnp.int32)
     cos_rows, sin_rows = turns(row_ids[:, None] * row_ids[None, :], n_rows, 1.0)
-    summed_re = jnp.einsum("ab,bcsu->csau", cos_rows, arrived[0], precision=highest) - jnp.einsum(
-        "ab,bcsu->csau", sin_rows, arrived[1], precision=highest
-    )
-    summed_im = jnp.einsum("ab,bcsu->csau", sin_rows, arrived[0], precision=highest) + jnp.einsum(
-        "ab,bcsu->csau", cos_rows, arrived[1], precision=highest
+    summed_re = jnp.einsum("ab,bcsu->csau", cos_rows, arrived[0], precision=three_pass) - jnp.einsum(
+        "ab,bcsu->csau", sin_rows, arrived[1], precision=three_pass
+    )
+    summed_im = jnp.einsum("ab,bcsu->csau", sin_rows, arrived[0], precision=three_pass) + jnp.einsum(
+        "ab,bcsu->csau", cos_rows, arrived[1], precision=three_pass
     )
     values = jnp.stack([summed_re, summed_im]).reshape(2, SEGMENTS, n_rows, small)
     leaf_count = n_rows * small

time: 384 us -> 368 us (0.958)
  matrix products: 159 us -> 144 us
    dot_general x22, matrix products: 122 us -> 107 us  [the longest x1 11 us: lift_dft(): jnp.einsum('jm,sxm->sjx', cos_two, section_re, precision=three_pass)]
  transfers between devices with their start and end apart: 5 -> 5, of which waited for: 3 -> 3; matrix products, arithmetic and copies ran while one was open for 8% -> 9% of each run, Pallas kernels for 0% -> 0%
where the time goes in v4:
time: 368 us; the launch traced here: 362 us
  matrix products  144 us (39%)
  waiting for transfers between devices  71.5 us (19%)
  local copies, waits for them, and re-layouts  64.8 us (18%)
  starting transfers between devices  33.9 us (9%)
  other arithmetic  28.5 us (8%)
  blocking collectives  18.1 us (5%)
    all_to_all x2, waiting for transfers between devices, regroup(): lax.all_to_all(values, ('rows', 'cols'), split_axis=1, concat_axis=1, til...  63.2 us
    dot_general x4, matrix products, permute(): jnp.dot(hash_mds, squash(state), precision=highest, preferred_element_typ...  20.8 us
    all_to_all x1, blocking collectives, regroup(): lax.all_to_all(values, ('rows', 'cols'), split_axis=1, concat_axis=1, til...  18.1 us
    unnamed x24, local copies, waits for them, and re-layouts  17.9 us
    all_to_all x2, starting transfers between devices, regroup(): lax.all_to_all(values, ('rows', 'cols'), split_axis=1, concat_axis=1, til...  15.9 us
    dot_general x1, matrix products, on_device(): jnp.dot(mds, trace, precision=highest, preferred_element_type=jnp.float32)  15.9 us
    all_to_all x1, starting transfers between devices, entering(): pieces = lax.all_to_all(spread, axis, 0, 0, tiled=True)  11.9 us
    dot_general x1, matrix products, lift_dft(): jnp.einsum('jm,sxm->sjx', cos_two, section_re, precision=three_pass)  11 us
  transfers between devices with their start and end apart: 5, of which 3 were waited for; matrix products, arithmetic and copies ran while one was open for 9% of the time, Pallas kernels for 0%

profile of v4, /device:TPU:1, one launch (start us, length us, event | category | flops | bytes accessed | tf_op | source)
XLA Modules:
  0.0 361.9 jit_solution(9622792201488669174)
XLA Ops:
  2.1 7.2 %constant_dynamic-update-slice_fusion.1 = f32[32,65544]{1,0:T(8,128)} fusion(f32[32,65536]{1,0:T(8,128)} %param.9), kind=kLoop, calls=%fused_computation.224 | loop fusion | bytes 16777216
  9.4 4.7 %convert_element_type.118 = f32[33,65536]{1,0:T(8,128)S(1)} convert(s32[33,65536]{1,0:T(8,128)} %param.10) | non-fusion elementwise | flops 2162688 | bytes 17301504 | tf_op jit(solution)/shard_map/convert_element_type | solution.py:149
  20.8 5.7 %log_subtract_fusion = (f32[1,65544]{1,0:T(1,128)S(1)}, f32[1,65544]{1,0:T(1,128)S(1)}, f32[1,65544]{1,0:T(1,128)S(1)}) fusion(f32[32,65544]{1,0:T(8,128)} %constant_dynamic-update-slice_fusion, f32[]{:T(128)} %bitcast.3, f32[]{:T(128)} %bitcast.2), kind=kLoop, calls=%fused_computation.140 | loop fusion | flops 589896 | bytes 1835240 | tf_op jit(solution)/shard_map/sub | solution.py:140
  35.1 11.9 %all-to-all-start = ((f32[128,1,1]{2,1,0:T(1,128)}), f32[128,1,1]{2,1,0:T(1,128)S(1)}, u32[]{:S(2)}, u32[]{:S(2)}) async-start(f32[128,1,1]{2,1,0:T(1,128)} %broadcast_in_dim.4), calls=%async_computation | async-start | bytes 131072 | tf_op jit(solution)/shard_map/all_to_all | solution.py:26
  47.0 15.9 %fusion.7 = f32[65536]{0:T(1024)S(1)} fusion(f32[32,65536]{1,0:T(8,128)} %param.9, f32[32,65544]{1,0:T(8,128)} %constant_dynamic-update-slice_fusion, f32[33,65536]{1,0:T(8,128)} %copy-done.2, f32[32]{0:T(128)S(1)} %copy-done.6, f32[32]{0:T(128)S(1)} %bitcast.183, f32[32,32]{1,0:T(8,128)S(1)} %copy-done), kind=kOutput, calls=%fused_computation.12 | convolution fusion | flops 819920896 | bytes 33820928 | tf_op jit(solution)/shard_map/dot_general | solution.py:134
  68.0 9.9 %all-to-all-start.1 = ((f32[1,128,512]{2,0,1:T(1,128)}), f32[1,128,512]{2,0,1:T(1,128)S(1)}, u32[]{:S(2)}, u32[]{:S(2)}) async-start(f32[1,128,512]{2,0,1:T(1,128)} %bitcast.19), calls=%async_computation.1 | async-start | bytes 524288 | tf_op jit(solution)/shard_map/all_to_all | solution.py:115
  77.9 10.8 %all-to-all-done.1 = f32[1,128,512]{2,0,1:T(1,128)S(1)} async-done(((f32[1,128,512]{2,0,1:T(1,128)}), f32[1,128,512]{2,0,1:T(1,128)S(1)}, u32[]{:S(2)}, u32[]{:S(2)}) %all-to-all-start.1) | async-done | bytes 262176 | tf_op jit(solution)/shard_map/all_to_all | solution.py:115
  91.5 18.1 %all_to_all.37 = f32[2,128,512]{2,0,1:T(2,128)S(1)} all-to-all(f32[2,128,512]{2,0,1:T(2,128)S(1)} %copy.48), channel_id=1, replica_groups=mesh['rows'=16,'cols'=8] {'rows','cols'}, dimensions={1} | all-to-all | bytes 1048576 | tf_op jit(solution)/shard_map/all_to_all | solution.py:115
  112.0 5.4 %fusion.79 = f32[512,128]{1,0:T(8,128)S(1)} fusion(f32[128,512]{1,0:T(8,128)S(1)} %convolution_add_fusion.6, f32[128,512]{1,0:T(8,128)S(1)} %convolution_subtract_fusion.2), kind=kOutput, calls=%fused_computation.119 | convolution fusion | flops 206110720 | bytes 786432 | tf_op jit(solution)/shard_map/...kn,jn->...kj/dot_general | solution.py:75
  117.4 5.8 %fusion.78 = f32[512,128]{1,0:T(8,128)S(1)} fusion(f32[128,512]{1,0:T(8,128)S(1)} %convolution_add_fusion.6, f32[128,512]{1,0:T(8,128)S(1)} %convolution_subtract_fusion.2), kind=kOutput, calls=%fused_computation.118 | convolution fusion | flops 206110720 | bytes 786432 | tf_op jit(solution)/shard_map/...kn,jn->...kj/dot_general | solution.py:72
  123.3 5.4 %fusion.61 = f32[512,128]{1,0:T(8,128)S(1)} fusion(f32[512,128]{1,0:T(8,128)S(1)} %fusion.79, f32[128,512]{1,0:T(8,128)S(1)} %convolution_add_fusion.6, f32[128,512]{1,0:T(8,128)S(1)} %convolution_subtract_fusion.2), kind=kOutput, calls=%fused_computation.95 | convolution fusion | flops 206241792 | bytes 1048576 | tf_op jit(solution)/shard_map/...kn,jn->...kj/dot_general | solution.py:75
  128.7 6.4 %fusion.62 = f32[512,128]{1,0:T(8,128)S(1)} fusion(f32[512,128]{1,0:T(8,128)S(1)} %fusion.78, f32[128,512]{1,0:T(8,128)S(1)} %convolution_add_fusion.6, f32[128,512]{1,0:T(8,128)S(1)} %convolution_subtract_fusion.2), kind=kOutput, calls=%fused_computation.97 | convolution fusion | flops 206241792 | bytes 1048576 | tf_op jit(solution)/shard_map/...kn,jn->...kj/dot_general | solution.py:72
  136.4 4.6 %all-to-all-start.3 = ((f32[2,8,1,8192]{3,0,2,1:T(2,128)}), f32[2,8,1,8192]{3,0,2,1:T(2,128)S(1)}, u32[]{:S(2)}, u32[]{:S(2)}) async-start(f32[2,8,1,8192]{3,0,2,1:T(2,128)} %copy.49), calls=%async_computation.3 | async-start | bytes 1048576 | tf_op jit(solution)/shard_map/all_to_all | solution.py:119
  142.1 8.3 %all-to-all-done.3 = f32[2,8,1,8192]{3,0,2,1:T(2,128)S(1)} async-done(((f32[2,8,1,8192]{3,0,2,1:T(2,128)}), f32[2,8,1,8192]{3,0,2,1:T(2,128)S(1)}, u32[]{:S(2)}, u32[]{:S(2)}) %all-to-all-start.3) | async-done | bytes 524320 | tf_op jit(solution)/shard_map/all_to_all | solution.py:119
  153.5 4.0 %mul.791 = f32[128,512]{1,0:T(8,128)S(1)} reshape(f32[1,1,8192,8]{3,2,1,0:T(8,128)} %copy.51) | data formatting | bytes 524288 | tf_op jit(solution)/shard_map/mul | solution.py:50
  164.1 8.6 %fusion.69 = f32[8,512,128]{1,2,0:T(8,128)S(1)} fusion(f32[128,512]{1,0:T(8,128)S(1)} %mul.791, s32[128,512]{1,0:T(8,128)S(1)} %multiply_add_fusion.6, f32[128,512]{1,0:T(8,128)S(1)} %mul.780), kind=kOutput, calls=%fused_computation.105 | convolution fusion | flops 411795456 | bytes 2883584 | tf_op jit(solution)/shard_map/kn,spnm->skpm/dot_general | solution.py:92
  172.7 9.0 %fusion.70 = f32[8,512,128]{1,2,0:T(8,128)S(1)} fusion(f32[128,512]{1,0:T(8,128)S(1)} %mul.791, s32[128,512]{1,0:T(8,128)S(1)} %multiply_add_fusion.6, f32[128,512]{1,0:T(8,128)S(1)} %mul.780), kind=kOutput, calls=%fused_computation.106 | convolution fusion | flops 411795456 | bytes 2883584 | tf_op jit(solution)/shard_map/kn,spnm->skpm/dot_general | solution.py:95
  181.7 8.9 %convolution_subtract_fusion.1 = f32[8,512,128]{1,2,0:T(8,128)S(1)} fusion(f32[8,512,128]{1,2,0:T(8,128)S(1)} %fusion.69, f32[128,512]{1,0:T(8,128)S(1)} %mul.791, s32[128,512]{1,0:T(8,128)S(1)} %multiply_add_fusion.6, f32[128,512]{1,0:T(8,128)S(1)} %mul.780), kind=kOutput, calls=%fused_computation.88 | convolution fusion | flops 412319744 | bytes 4980736 | tf_op jit(solution)/shard_map/kn,spnm->skpm/dot_general | solution.py:92
  190.6 9.8 %fusion.34 = (f32[1,128,8,512]{3,1,2,0:T(8,128)S(1)}, f32[1,128,8,512]{3,1,2,0:T(8,128)S(1)}) fusion(f32[8,512,128]{1,2,0:T(8,128)S(1)} %convolution_subtract_fusion.1, f32[128,512]{1,0:T(8,128)S(1)} %get-tuple-element.32, f32[128,512]{1,0:T(8,128)S(1)} %get-tuple-element.33, f32[8,512,128]{1,2,0:T(8,128)S(1)} %fusion.70, f32[128,512]{1,0:T(8,128)S(1)} %mul.791, ...), kind=kOutput, calls=%fused_computation.56 | convolution fusion | flops 415465472 | bytes 9699328 | tf_op jit(solution)/shard_map/kn,spnm->skpm/dot_general | solution.py:95
  200.4 6.2 %fusion.30 = f32[1024,512]{1,0:T(8,128)S(1)} fusion(f32[1,128,8,512]{3,1,2,0:T(8,128)S(1)} %get-tuple-element.9), kind=kOutput, calls=%fused_computation.50 | convolution fusion | flops 1614282752 | bytes 4194304 | tf_op jit(solution)/shard_map/jm,sxm->sjx/dot_general | solution.py:108
  206.6 9.1 %fusion.32 = f32[1024,512]{1,0:T(8,128)} fusion(f32[1,128,8,512]{3,1,2,0:T(8,128)S(1)} %get-tuple-element.9), kind=kOutput, calls=%fused_computation.52 | convolution fusion | flops 1614282752 | bytes 4194304 | tf_op jit(solution)/shard_map/jm,sxm->sjx/dot_general | solution.py:105
  215.7 9.2 %add_bitcast_fusion = f32[1,512,1024]{1,2,0:T(8,128)} fusion(f32[1024,512]{1,0:T(8,128)S(1)} %fusion.30, f32[1,128,8,512]{3,1,2,0:T(8,128)S(1)} %get-tuple-element.8), kind=kOutput, calls=%fused_computation.70 | convolution fusion | flops 1614807040 | bytes 6291456 | tf_op jit(solution)/shard_map/jm,sxm->sjx/dot_general | solution.py:108
  228.9 11.0 %subtract_bitcast_fusion = f32[1,512,1024]{1,2,0:T(8,128)} fusion(f32[1024,512]{1,0:T(8,128)} %fusion.32, f32[1,128,8,512]{3,1,2,0:T(8,128)} %copy-done.8), kind=kOutput, calls=%fused_computation.71 | convolution fusion | flops 1614807040 | bytes 6291456 | tf_op jit(solution)/shard_map/jm,sxm->sjx/dot_general | solution.py:105
  243.8 10.2 %multiply_subtract_fusion = (f32[1,128,1,4096]{3,1,2,0:T(8,128)S(1)}, f32[1,128,1,4096]{3,1,2,0:T(8,128)S(1)}) fusion(f32[1,128,1,4096]{3,1,2,0:T(8,128)} %reshape.486, f32[1,128,1,4096]{3,1,2,0:T(8,128)} %reshape.485, s32[]{:T(128)S(6)} %axis_index.17), kind=kLoop, calls=%fused_computation.69 | loop fusion | flops 11534336 | bytes 8388612 | tf_op jit(solution)/shard_map/sub | solution.py:50
  254.3 6.3 %copy.56 = f32[2,128,1,4096]{3,2,0,1:T(1,128)} copy(f32[2,128,1,4096]{3,1,2,0:T(8,128)S(1)} %pad_maximum_fusion) | data formatting | bytes 8388608 | tf_op jit(solution)/shard_map/stack | solution.py:193
  260.6 6.0 %all-to-all-start.4 = ((f32[2,128,1,4096]{3,2,0,1:T(1,128)}), f32[2,128,1,4096]{3,2,0,1:T(1,128)}, u32[]{:S(2)}, u32[]{:S(2)}) async-start(f32[2,128,1,4096]{3,2,0,1:T(1,128)} %copy.56), calls=%async_computation.4 | async-start | bytes 8388608 | tf_op jit(solution)/shard_map/all_to_all | solution.py:115
  266.7 52.4 %all-to-all-done.4 = f32[2,128,1,4096]{3,2,0,1:T(1,128)} async-done(((f32[2,128,1,4096]{3,2,0,1:T(1,128)}), f32[2,128,1,4096]{3,2,0,1:T(1,128)}, u32[]{:S(2)}, u32[]{:S(2)}) %all-to-all-start.4) | async-done | bytes 4194336 | tf_op jit(solution)/shard_map/all_to_all | solution.py:115
  319.1 6.0 %fusion.290 = (f32[1,128,1,4096]{3,2,0,1:T(1,128)S(1)}, f32[1,128,1,4096]{3,2,0,1:T(1,128)S(1)}) fusion(f32[2,128,1,4096]{3,2,0,1:T(1,128)} %all-to-all-done.4), kind=kLoop, calls=%fused_computation.352 | loop fusion | bytes 8388608 | tf_op jit(solution)/shard_map/slice | solution.py:201
  339.1 5.3 %fusion.4 = f32[12,65536]{1,0:T(8,128)S(1)} fusion(f32[12,12]{1,0:T(8,128)S(1)} %copy-done.3, f32[8,65536]{1,0:T(8,128)S(1)} %bitcast.167, f32[12]{0:T(128)S(1)} %get-tuple-element.29), kind=kOutput, calls=%fused_computation.8 | convolution fusion | flops 116391936 | bytes 5243504 | tf_op jit(solution)/shard_map/dot_general | solution.py:38
  344.4 5.6 %fusion.3 = f32[12,65536]{1,0:T(8,128)S(1)} fusion(f32[12,12]{1,0:T(8,128)S(1)} %copy-done.3, f32[8,65536]{1,0:T(8,128)S(1)} %bitcast.163, f32[12,65536]{1,0:T(8,128)S(1)} %fusion.4, f32[12]{0:T(128)S(1)} %get-tuple-element.28), kind=kOutput, calls=%fused_computation.6 | convolution fusion | flops 117178368 | bytes 8389232 | tf_op jit(solution)/shard_map/dot_general | solution.py:38
  350.0 5.0 %fusion.1 = f32[12,65536]{1,0:T(8,128)S(1)} fusion(f32[12,12]{1,0:T(8,128)S(1)} %copy-done.3, f32[12,65536]{1,0:T(8,128)S(1)} %fusion.3, f32[12]{0:T(128)S(1)} %get-tuple-element.29), kind=kOutput, calls=%fused_computation.3 | convolution fusion | flops 116391936 | bytes 6292080 | tf_op jit(solution)/shard_map/dot_general | solution.py:38
  355.0 5.0 %fusion = f32[12,65536]{1,0:T(8,128)S(1)} fusion(f32[12,12]{1,0:T(8,128)S(1)} %copy-done.3, f32[12,65536]{1,0:T(8,128)S(1)} %fusion.1, f32[12]{0:T(128)S(1)} %get-tuple-element.28), kind=kOutput, calls=%fused_computation.1 | convolution fusion | flops 116391936 | bytes 6292080 | tf_op jit(solution)/shard_map/dot_general | solution.py:38
  (83 shorter events, 62.8 us)
Async XLA Ops:
  0.0 47.0 %copy-start = (f32[32,32]{1,0:T(8,128)S(1)}, f32[32,32]{1,0:T(8,128)}, u32[]{:S(2)}) copy-start(f32[32,32]{1,0:T(8,128)} %param.11) | copy-start | bytes 12292
  0.7 19.4 %collective-permute-start = (f32[32,8]{1,0:T(8,128)S(1)}, f32[32,8]{1,0:T(8,128)S(1)}, u32[]{:S(2)}, u32[]{:S(2)}) collective-permute-start(f32[32,8]{1,0:T(8,128)S(1)} %slice.131), channel_id=1, source_target_pairs={{0,127},{1,0},{2,1},{3,2},{4,3},{5,4},{6,5},{7,6},{8,7},{9,8},{10,... | collective-permute-start | bytes 3080 | tf_op jit(solution)/shard_map/ppermute | solution.py:20
  9.3 4.7 %copy-start.7 = (f32[33]{0:T(128)S(1)}, f32[33]{0:T(128)}, u32[]{:S(2)}) copy-start(f32[33]{0:T(128)} %param.13) | copy-start | bytes 400
  9.3 9.5 %copy-start.4 = (f32[2]{0:T(128)S(1)}, f32[2]{0:T(128)}, u32[]{:S(2)}) copy-start(f32[2]{0:T(128)} %param.14) | copy-start | bytes 28
  14.0 4.0 %copy-start.2 = (f32[33,65536]{1,0:T(8,128)}, f32[33,65536]{1,0:T(8,128)S(1)}, u32[]{:S(2)}) copy-start(f32[33,65536]{1,0:T(8,128)S(1)} %convert_element_type.118) | copy-start | bytes 25952260
  30.3 16.7 %copy-start.6 = (f32[32]{0:T(128)S(1)}, f32[32]{0:T(128)}, u32[]{:S(2)}) copy-start(f32[32]{0:T(128)} %param.12) | copy-start | bytes 388
  35.1 28.6 %all-to-all-start = ((f32[128,1,1]{2,1,0:T(1,128)}), f32[128,1,1]{2,1,0:T(1,128)S(1)}, u32[]{:S(2)}, u32[]{:S(2)}) async-start(f32[128,1,1]{2,1,0:T(1,128)} %broadcast_in_dim.4), calls=%async_computation | async-start | bytes 131072 | tf_op jit(solution)/shard_map/all_to_all | solution.py:26
  68.0 20.7 %all-to-all-start.1 = ((f32[1,128,512]{2,0,1:T(1,128)}), f32[1,128,512]{2,0,1:T(1,128)S(1)}, u32[]{:S(2)}, u32[]{:S(2)}) async-start(f32[1,128,512]{2,0,1:T(1,128)} %bitcast.19), calls=%async_computation.1 | async-start | bytes 524288 | tf_op jit(solution)/shard_map/all_to_all | solution.py:115
  136.4 14.0 %all-to-all-start.3 = ((f32[2,8,1,8192]{3,0,2,1:T(2,128)}), f32[2,8,1,8192]{3,0,2,1:T(2,128)S(1)}, u32[]{:S(2)}, u32[]{:S(2)}) async-start(f32[2,8,1,8192]{3,0,2,1:T(2,128)} %copy.49), calls=%async_computation.3 | async-start | bytes 1048576 | tf_op jit(solution)/shard_map/all_to_all | solution.py:119
  200.4 15.4 %copy-start.8 = (f32[1,128,8,512]{3,1,2,0:T(8,128)}, f32[1,128,8,512]{3,1,2,0:T(8,128)S(1)}, u32[]{:S(2)}) copy-start(f32[1,128,8,512]{3,1,2,0:T(8,128)S(1)} %get-tuple-element.8) | copy-start | bytes 6291460
  260.6 6.1 %copy-start.5 = (f32[2,12]{1,0:T(2,128)S(1)}, f32[2,12]{1,0:T(2,128)}, u32[]{:S(2)}) copy-start(f32[2,12]{1,0:T(2,128)} %param.17) | copy-start | bytes 292
  260.6 58.5 %all-to-all-start.4 = ((f32[2,128,1,4096]{3,2,0,1:T(1,128)}), f32[2,128,1,4096]{3,2,0,1:T(1,128)}, u32[]{:S(2)}, u32[]{:S(2)}) async-start(f32[2,128,1,4096]{3,2,0,1:T(1,128)} %copy.56), calls=%async_computation.4 | async-start | bytes 8388608 | tf_op jit(solution)/shard_map/all_to_all | solution.py:115
  337.9 1.2 copy-start.3
  355.0 6.7 %copy-start.1 = (f32[32,32]{1,0:T(8,128)S(1)}, f32[32,32]{1,0:T(8,128)}, u32[]{:S(2)}) copy-start(f32[32,32]{1,0:T(8,128)} %param.11) | copy-start | bytes 12292
